TPU v7x, 32 devices: a whole 2x2x4 slice. The times are simulated.
32 devices in a mesh: rows: 8 (over z, y), heads: 4 (over x, core).
Axes of the slice: x: 2, y: 2, z: 4, core: 2. Of those that a mesh axis runs over, the one named last changes fastest.
Arguments:
- hidden_in: bfloat16 [32768, 768], P(('rows', 'heads')), may hold values from -6 to 6
- cotangent: bfloat16 [32768, 768], P(('rows', 'heads')), may hold values from -6 to 6
- part_lengths: int32 [32, 2], P('rows'), may hold values from 1 to 512, as said below
- segment_start: int32 [32], P('rows'), may hold values from 1 to 1023, as said below
- query_weight: bfloat16 [768, 768], replicated, may hold values from -0.21875 to 0.21875
- value_weight: bfloat16 [768, 768], replicated, may hold values from -0.21875 to 0.21875
- shared_down: bfloat16 [768, 1024], replicated, may hold values from -0.21875 to 0.21875
- shared_up: bfloat16 [1024, 768], replicated, may hold values from -0.1875 to 0.1875
- owner: int32 [640], replicated, may hold values from 0 to 31, as said below
- weights: float32 [15360, 768], P(('rows', 'heads'))
- first_moment: float32 [15360, 768], P(('rows', 'heads'))
- second_moment: float32 [15360, 768], P(('rows', 'heads')), as said below
- small_weights: float32 [11264], P(('rows', 'heads'))
- small_first: float32 [11264], P(('rows', 'heads'))
- small_second: float32 [11264], P(('rows', 'heads')), as said below
Outputs:
- block_out: bfloat16 [32768, 768], P(('rows', 'heads'))
- input_grad: bfloat16 [32768, 768], P(('rows', 'heads'))
- new_weights: float32 [15360, 768], P(('rows', 'heads'))
- new_first: float32 [15360, 768], P(('rows', 'heads'))
- new_second: float32 [15360, 768], P(('rows', 'heads'))
- weights_copy: bfloat16 [15360, 768], P(('rows', 'heads'))
- new_small: float32 [11264], P(('rows', 'heads'))
- new_small_first: float32 [11264], P(('rows', 'heads'))
- new_small_second: float32 [11264], P(('rows', 'heads'))
- small_copy: bfloat16 [11264], P(('rows', 'heads'))
Inputs may be any that keep to these rules, and one draw needn't show every extreme that they name: Part one holds positions 0 to part_lengths[s, 0] - 1; some sequence has a part of exactly 512 tokens. part_lengths[s, 0] <= segment_start[s] and segment_start[s] + part_lengths[s, 1] <= 1024; other positions are padding. `owner`: no device owns more than 40 blocks, and some device owns exactly 40. `second_moment`: entries are positive. `small_second`: entries are positive.
All inputs are finite; a program needn't handle non-finite values.
Results may differ from a plain program's by a relative error of at most 0.015.
The roundings to bfloat16 on the way count: a program that leaves them out, or rounds other values in their place, can miss the bound.
Values may be sent and summed in bfloat16 or wider, within the bound.
No kernel may reach another device: no remote copies, remote signals or barrier semaphores. Data moves between devices by JAX's collectives and lax.ppermute only.
A program may use at most 256 MiB of HBM per device.

v0:
```python
import jax
import jax.numpy as jnp
from jax import lax
from jax.sharding import PartitionSpec as P

D = 768
FF = 3072
HEAD_DIM = 64
RANK = 1024
SEQ_LEN = 1024
STEP = 3
BLOCK_ROWS = 12


def slot_index(owner, capacity):
    count = owner.shape[0]
    order = jnp.arange(count, dtype=jnp.int32)
    same_owner = owner[:, None] == owner[None, :]
    earlier = order[None, :] < order[:, None]
    ranked = jnp.sum((same_owner & earlier).astype(jnp.int32), axis=1)
    return owner * capacity + ranked


def slot_source(slot, slot_count):
    blocks = slot.shape[0]
    match = slot[None, :] == jnp.arange(slot_count, dtype=jnp.int32)[:, None]
    source = jnp.sum(match.astype(jnp.int32) * jnp.arange(blocks, dtype=jnp.int32)[None, :], axis=1)
    filled = jnp.any(match, axis=1)
    return (source, filled)


def split_small(vector):
    widths = [RANK, RANK, D, D, D, FF, D, D, D, D, D]
    pieces = []
    offset = 0
    for width in widths:
        pieces.append(vector[offset : offset + width])
        offset = offset + width
    return pieces


def unpack_rows(gathered, slot):
    rows = gathered.reshape(-1, BLOCK_ROWS, D)[slot].reshape(-1, D)
    return (rows[:D], rows[D : 2 * D], rows[2 * D : 2 * D + FF], rows[2 * D + FF :])


def visibility(lengths, starts):
    places = jnp.arange(SEQ_LEN, dtype=jnp.int32)[None, :]
    first_len = lengths[:, 0:1]
    second_len = lengths[:, 1:2]
    begin = starts[:, None]
    return (places < first_len) | (places >= begin) & (places < begin + second_len)


def product(left, right):
    return jnp.dot(left, right, preferred_element_type=jnp.float32)


def product_t(left, right):
    return lax.dot_general(
        left, right, (((1,), (1,)), ((), ())), preferred_element_type=jnp.float32
    )


def inner_rows(left, right):
    return lax.dot_general(
        left, right, (((0,), (0,)), ((), ())), preferred_element_type=jnp.float32
    )


def normalize(values):
    centre = jnp.mean(values, axis=-1, keepdims=True)
    centred = values - centre
    spread = jnp.mean(centred * centred, axis=-1, keepdims=True)
    inverse = lax.rsqrt(spread + 1e-05)
    return (centred * inverse, inverse)


def norm_back(grad_norm, normed, inverse):
    first_mean = jnp.mean(grad_norm, axis=-1, keepdims=True)
    second_mean = jnp.mean(grad_norm * normed, axis=-1, keepdims=True)
    return inverse * (grad_norm - first_mean - normed * second_mean)


def gelu_slope(values):
    return (
        0.5 * (1.0 + jax.scipy.special.erf(values * 0.7071067811865476))
        + values * jnp.exp(-0.5 * values * values) * 0.3989422804014327
    )


def masked_scores(query, keys, visible):
    scores = jnp.einsum("qhd,khd->hqk", query, keys, preferred_element_type=jnp.float32) * 0.125
    return jnp.where(visible[None, None, :], scores, -1e30)


def attend_forward(pieces):
    query, keys, values, visible = pieces
    scores = masked_scores(query, keys, visible)
    highest = jnp.max(scores, axis=-1, keepdims=True)
    raised = jnp.exp(scores - highest)
    summed = jnp.sum(raised, axis=-1, keepdims=True)
    probs = raised / summed
    context = jnp.einsum(
        "hqk,khd->qhd", probs.astype(jnp.bfloat16), values, preferred_element_type=jnp.float32
    )
    return (context.astype(jnp.bfloat16), highest[..., 0] + jnp.log(summed[..., 0]))


def attend_backward(pieces):
    query, keys, values, visible, log_total, grad_context = pieces
    scores = masked_scores(query, keys, visible)
    probs = jnp.exp(scores - log_total[..., None])
    probs_low = probs.astype(jnp.bfloat16)
    grad_values = jnp.einsum(
        "hqk,qhd->khd", probs_low, grad_context, preferred_element_type=jnp.float32
    )
    grad_probs = jnp.einsum(
        "qhd,khd->hqk", grad_context, values, preferred_element_type=jnp.float32
    )
    row_dot = jnp.sum(probs * grad_probs, axis=-1, keepdims=True)
    grad_scores = (probs * (grad_probs - row_dot)).astype(jnp.bfloat16)
    grad_query = (
        jnp.einsum("hqk,khd->qhd", grad_scores, keys, preferred_element_type=jnp.float32) * 0.125
    )
    grad_keys = (
        jnp.einsum("hqk,qhd->khd", grad_scores, query, preferred_element_type=jnp.float32) * 0.125
    )
    return (
        grad_query.astype(jnp.bfloat16),
        grad_keys.astype(jnp.bfloat16),
        grad_values.astype(jnp.bfloat16),
    )


def adamw_update(master, first, second, grad, decay, rate):
    correct = 1.0 - 0.5**STEP
    first_new = 0.5 * first + 0.5 * grad
    second_new = 0.5 * second + 0.5 * grad * grad
    update = first_new / correct / (jnp.sqrt(second_new / correct) + 1e-08) + decay * master
    return (master - rate * update, first_new, second_new)


def body(
    hidden_in,
    cotangent,
    part_lengths,
    segment_start,
    query_weight,
    value_weight,
    shared_down,
    shared_up,
    owner,
    weights,
    first_moment,
    second_moment,
    small_weights,
    small_first,
    small_second,
):
    capacity = weights.shape[0] // BLOCK_ROWS
    devices = lax.axis_size("rows") * lax.axis_size("heads")
    slot = slot_index(owner, capacity)
    gathered, small_all = (
        lax.all_gather(weights.astype(jnp.bfloat16), ("rows", "heads"), axis=0, tiled=True),
        lax.all_gather(small_weights.astype(jnp.bfloat16), ("rows", "heads"), axis=0, tiled=True),
    )
    key_rows, out_rows, up_rows, down_rows = unpack_rows(gathered, slot)
    (
        scale_q_rank,
        scale_v_rank,
        scale_q_out,
        scale_v_out,
        out_bias,
        up_bias,
        down_bias,
        gain_one,
        shift_one,
        gain_two,
        shift_two,
    ) = [piece.astype(jnp.float32) for piece in split_small(small_all)]
    projected = product(hidden_in, shared_down).astype(jnp.bfloat16)
    projected_wide = projected.astype(jnp.float32)
    rank_q = (scale_q_rank * projected_wide).astype(jnp.bfloat16)
    rank_v = (scale_v_rank * projected_wide).astype(jnp.bfloat16)
    side_q = product(rank_q, shared_up)
    side_v = product(rank_v, shared_up)
    query = (product(hidden_in, query_weight) + scale_q_out * side_q).astype(jnp.bfloat16)
    keys = product(hidden_in, key_rows).astype(jnp.bfloat16)
    values = (product(hidden_in, value_weight) + scale_v_out * side_v).astype(jnp.bfloat16)
    query_h, keys_h, values_h = (
        lax.all_to_all(query, "heads", split_axis=1, concat_axis=0, tiled=True),
        lax.all_to_all(keys, "heads", split_axis=1, concat_axis=0, tiled=True),
        lax.all_to_all(values, "heads", split_axis=1, concat_axis=0, tiled=True),
    )
    local = query_h.shape[1] // HEAD_DIM
    head_shape = (-1, SEQ_LEN, local, HEAD_DIM)
    query_h = query_h.reshape(head_shape)
    keys_h = keys_h.reshape(head_shape)
    values_h = values_h.reshape(head_shape)
    visible = visibility(part_lengths, segment_start)

    def forward_step(carry, pieces):
        return (carry, attend_forward(pieces))

    _, (context_h, log_total) = lax.scan(forward_step, 0, (query_h, keys_h, values_h, visible))
    context = lax.all_to_all(
        context_h.reshape(-1, local * HEAD_DIM), "heads", split_axis=0, concat_axis=1, tiled=True
    )
    attended = product(context, out_rows) + out_bias
    first_sum = hidden_in.astype(jnp.float32) + attended
    norm_one, inverse_one = normalize(first_sum)
    hidden_one = norm_one * gain_one + shift_one
    hidden_low = hidden_one.astype(jnp.bfloat16)
    pre_act = product_t(hidden_low, up_rows) + up_bias
    active = jax.nn.gelu(pre_act, approximate=False).astype(jnp.bfloat16)
    second_sum = hidden_one + product(active, down_rows) + down_bias
    norm_two, inverse_two = normalize(second_sum)
    block_out = (norm_two * gain_two + shift_two).astype(jnp.bfloat16)
    regathered = lax.all_gather(weights.astype(jnp.bfloat16), ("rows", "heads"), axis=0, tiled=True)
    key_rows, out_rows, up_rows, down_rows = unpack_rows(regathered, slot)
    grad_top = cotangent.astype(jnp.float32)
    grad_gain_two = jnp.sum(grad_top * norm_two, axis=0)
    grad_shift_two = jnp.sum(grad_top, axis=0)
    grad_second = norm_back(grad_top * gain_two, norm_two, inverse_two)
    grad_branch = grad_second.astype(jnp.bfloat16)
    grad_down_bias = jnp.sum(grad_branch.astype(jnp.float32), axis=0)
    grad_down = inner_rows(active, grad_branch)
    grad_pre = (product_t(grad_branch, down_rows) * gelu_slope(pre_act)).astype(jnp.bfloat16)
    grad_up_bias = jnp.sum(grad_pre.astype(jnp.float32), axis=0)
    grad_up = inner_rows(grad_pre, hidden_low)
    grad_hidden = grad_second + product(grad_pre, up_rows)
    grad_gain_one = jnp.sum(grad_hidden * norm_one, axis=0)
    grad_shift_one = jnp.sum(grad_hidden, axis=0)
    grad_first = norm_back(grad_hidden * gain_one, norm_one, inverse_one)
    grad_attended = grad_first.astype(jnp.bfloat16)
    grad_out_bias = jnp.sum(grad_attended.astype(jnp.float32), axis=0)
    grad_out = inner_rows(context, grad_attended)
    grad_context = product_t(grad_attended, out_rows).astype(jnp.bfloat16)
    grad_context_h = lax.all_to_all(
        grad_context, "heads", split_axis=1, concat_axis=0, tiled=True
    ).reshape(head_shape)

    def backward_step(carry, pieces):
        return (carry, attend_backward(pieces))

    _, (grad_query_h, grad_keys_h, grad_values_h) = lax.scan(
        backward_step, 0, (query_h, keys_h, values_h, visible, log_total, grad_context_h)
    )
    flat_width = local * HEAD_DIM
    grad_query, grad_keys, grad_values = (
        lax.all_to_all(
            grad_query_h.reshape(-1, flat_width), "heads", split_axis=0, concat_axis=1, tiled=True
        ),
        lax.all_to_all(
            grad_keys_h.reshape(-1, flat_width), "heads", split_axis=0, concat_axis=1, tiled=True
        ),
        lax.all_to_all(
            grad_values_h.reshape(-1, flat_width), "heads", split_axis=0, concat_axis=1, tiled=True
        ),
    )
    grad_key = inner_rows(hidden_in, grad_keys)
    grad_query_wide = grad_query.astype(jnp.float32)
    grad_values_wide = grad_values.astype(jnp.float32)
    grad_scale_q_out = jnp.sum(grad_query_wide * side_q, axis=0)
    grad_scale_v_out = jnp.sum(grad_values_wide * side_v, axis=0)
    grad_side_q = (scale_q_out * grad_query_wide).astype(jnp.bfloat16)
    grad_side_v = (scale_v_out * grad_values_wide).astype(jnp.bfloat16)
    grad_rank_q = product_t(grad_side_q, shared_up)
    grad_rank_v = product_t(grad_side_v, shared_up)
    grad_scale_q_rank = jnp.sum(grad_rank_q * projected_wide, axis=0)
    grad_scale_v_rank = jnp.sum(grad_rank_v * projected_wide, axis=0)
    grad_projected = (grad_rank_q * scale_q_rank + grad_rank_v * scale_v_rank).astype(jnp.bfloat16)
    grad_input = grad_first + product_t(grad_query, query_weight) + product_t(grad_keys, key_rows)
    grad_input = (
        grad_input + product_t(grad_values, value_weight) + product_t(grad_projected, shared_down)
    )
    input_grad = grad_input.astype(jnp.bfloat16)
    grad_rows = jnp.concatenate([grad_key, grad_out, grad_up, grad_down], axis=0).reshape(
        -1, BLOCK_ROWS, D
    )
    source, filled = slot_source(slot, devices * capacity)
    small_grad = jnp.concatenate(
        [
            grad_scale_q_rank,
            grad_scale_v_rank,
            grad_scale_q_out,
            grad_scale_v_out,
            grad_out_bias,
            grad_up_bias,
            grad_down_bias,
            grad_gain_one,
            grad_shift_one,
            grad_gain_two,
            grad_shift_two,
        ]
    )
    slotted = (grad_rows[source] * filled.astype(jnp.float32)[:, None, None]).reshape(-1, D)
    owned_grad, owned_small = (
        lax.psum_scatter(slotted, ("rows", "heads"), scatter_dimension=0, tiled=True),
        lax.psum_scatter(small_grad, ("rows", "heads"), scatter_dimension=0, tiled=True),
    )
    new_weights, new_first, new_second = adamw_update(
        weights, first_moment, second_moment, owned_grad, 0.01, 0.03
    )
    new_small, new_small_first, new_small_second = adamw_update(
        small_weights, small_first, small_second, owned_small, 0.0, 0.3
    )
    return (
        block_out,
        input_grad,
        new_weights,
        new_first,
        new_second,
        new_weights.astype(jnp.bfloat16),
        new_small,
        new_small_first,
        new_small_second,
        new_small.astype(jnp.bfloat16),
    )


def solution(mesh):
    return jax.shard_map(
        body,
        mesh=mesh,
        in_specs=(
            P(("rows", "heads"), None),
            P(("rows", "heads"), None),
            P("rows", None),
            P("rows"),
            P(),
            P(),
            P(),
            P(),
            P(),
            P(("rows", "heads"), None),
            P(("rows", "heads"), None),
            P(("rows", "heads"), None),
            P(("rows", "heads")),
            P(("rows", "heads")),
            P(("rows", "heads")),
        ),
        out_specs=(
            P(("rows", "heads"), None),
            P(("rows", "heads"), None),
            P(("rows", "heads"), None),
            P(("rows", "heads"), None),
            P(("rows", "heads"), None),
            P(("rows", "heads"), None),
            P(("rows", "heads")),
            P(("rows", "heads")),
            P(("rows", "heads")),
            P(("rows", "heads")),
        ),
        check_vma=False,
    )
```

profile of v0, /device:TPU:0, one launch (start us, length us, event | category | flops | bytes accessed | tf_op | source)
XLA Modules:
  0.0 1231.7 jit_solution(16424959777222221229)
XLA Ops:
  10.6 44.2 %all-reduce = bf16[11264]{0:T(1024)(128)(2,1)S(1)} all-reduce(bf16[11264]{0:T(1024)(128)(2,1)S(1)} %dynamic-update-slice), channel_id=1, replica_groups=mesh['rows'=8,'heads'=4] {'rows','heads'}, use_global_device_ids=true, to_apply=%add | all-reduce | flops 11264 | bytes 45056
  75.8 13.4 %all-to-all-done.1 = bf16[1024,4,192]{0,2,1:T(8,128)(2,1)S(1)} async-done(((bf16[1024,4,192]{0,2,1:T(8,128)(2,1)}), bf16[1024,4,192]{0,2,1:T(8,128)(2,1)S(1)}, u32[]{:S(2)}, u32[]{:S(2)}) %all-to-all-start.1) | async-done | bytes 1572896 | tf_op jit(solution)/shard_map/all_to_all | solution.py:192
  94.1 86.6 %all-gather.2.cloned.1.call-done = bf16[15360,768]{1,0:T(8,128)(2,1)} async-done(((bf16[480,768]{1,0:T(8,128)(2,1)}), bf16[15360,768]{1,0:T(8,128)(2,1)}) %all-gather.2.cloned.1.call-update) | async-done | bytes 23592976 | tf_op jit(solution)/shard_map/all_gather | solution.py:165
  180.7 36.1 %reshape.182 = bf16[1280,12,768]{2,1,0:T(8,128)(2,1)} reshape(bf16[15360,768]{1,0:T(8,128)(2,1)} %all-gather.2.cloned.1.call-done) | data formatting | bytes 47185920 | tf_op jit(solution)/shard_map/reshape | solution.py:43
  216.7 29.4 %gather_fusion = bf16[640,12,768]{2,1,0:T(8,128)(2,1)} fusion(bf16[1280,12,768]{2,1,0:T(8,128)(2,1)} %reshape.182, s32[1024]{0:T(1024)S(1)} %pad_clamp_fusion.1), kind=kCustom, calls=%fused_computation | custom fusion | bytes 23595520 | tf_op jit(solution)/shard_map/gather | solution.py:43
  271.2 11.1 all-to-all-done.2
  283.6 49.7 %while.26 = (s32[]{:T(128)}, bf16[4,1024,3,64]{1,3,2,0:T(8,128)(2,1)}, f32[4,3,1024]{2,1,0:T(4,128)}, bf16[4,1024,3,64]{1,3,2,0:T(8,128)(2,1)}, pred[4,1024]{1,0...) while((s32[]{:T(128)}, ...), condition=%wide.region_4.5_spmd, body=%wide.region_1.4_spmd.sunk | while | flops 843248640 | bytes 39431268 | solution.py:206
  339.4 10.4 fusion.127
  349.8 8.5 slice.84
  372.3 35.6 %fusion.61 = (bf16[1024,3072]{1,0:T(8,128)(2,1)}, f32[1024,3072]{1,0:T(8,128)}) fusion(f32[3072]{0:T(1024)S(1)} %slice_convert_fusion, bf16[3072,768]{1,0:T(8,128)(2,1)S(1)} %bitcast.188, f32[1024,768]{0,1:T(8,128)S(1)} %get-tuple-element.227, f32[768]{0:T(1024)S(1)} %copy-done.52, f32[768]{0:T(1024)S(1)} %copy-done.42, f32[1024]{0:T(1024)S(1)} %add_rsqrt_fusion.1, ...), kind=kOutput, calls=%fused_computation.72 | convolution fusion | flops 5043388416 | bytes 26765312 | tf_op jit(solution)/shard_map/dot_general | solution.py:60
  422.2 14.7 %convert_reduce_fusion = (f32[3072]{0:T(1024)}, bf16[1024,3072]{1,0:T(8,128)(2,1)}) fusion(f32[1024,3072]{1,0:T(8,128)} %get-tuple-element.229, f32[3072]{0:T(1024)S(1)} %slice_convert_fusion, bf16[1024,768]{0,1:T(8,128)(2,1)S(1)} %get-tuple-element.196, bf16[3072,768]{1,0:T(8,128)(2,1)S(1)} %bitcast.190), kind=kOutput, calls=%fused_computation.79 | convolution fusion | flops 4872729600 | bytes 25190400 | tf_op jit(solution)/shard_map/dot_general | solution.py:60
  436.8 10.8 multiply_reduce_fusion.1
  458.3 11.1 fusion.118
  482.4 112.6 %while.27 = (s32[]{:T(128)}, bf16[4,1024,3,64]{1,3,2,0:T(8,128)(2,1)}, bf16[4,1024,3,64]{1,3,2,0:T(8,128)(2,1)}, bf16[4,1024,3,64]{1,3,2,0:T(8,128)(2,1)}, bf16[...) while((s32[]{:T(128)}, ...), condition=%wide.region_15.16_spmd, body=%wide.region_13.15_spmd.sunk | while | flops 2061431808 | bytes 123566232 | solution.py:247
  599.4 10.2 fusion.131
  609.6 9.9 all-to-all-done.6
  624.3 12.3 pad_maximum_fusion
  636.6 26.9 %reshape.185 = f32[640,12,768]{2,1,0:T(8,128)} reshape(f32[7680,768]{1,0:T(8,128)} %pad_maximum_fusion) | data formatting | bytes 47185920 | tf_op jit(solution)/shard_map/reshape | solution.py:279
  663.5 60.2 %gather_fusion.1 = f32[1280,12,768]{2,1,0:T(8,128)} fusion(f32[640,12,768]{2,1,0:T(8,128)} %reshape.185, s32[2048]{0:T(1024)S(1)} %copy-done.39), kind=kCustom, calls=%fused_computation.1 | custom fusion | bytes 94376960 | tf_op jit(solution)/shard_map/gather | solution.py:298
  723.8 54.9 %gather.11 = f32[15360,768]{1,0:T(8,128)} reshape(f32[1280,12,768]{2,1,0:T(8,128)} %gather_fusion.1) | data formatting | bytes 94371840 | tf_op jit(solution)/shard_map/gather | solution.py:298
  778.6 31.1 %broadcast_multiply_fusion = f32[15360,768]{1,0:T(8,128)} fusion(f32[15360,768]{1,0:T(8,128)} %gather.11, f32[15360]{0:T(1024)S(1)} %copy-done.31), kind=kLoop, calls=%fused_computation.67 | loop fusion | flops 11796480 | bytes 94433280 | tf_op jit(solution)/shard_map/mul | solution.py:298
  815.8 18.5 %all-to-all-done.5 = bf16[4,1024,192]{1,2,0:T(8,128)(2,1)} async-done(((bf16[4,1024,192]{1,2,0:T(8,128)(2,1)}), bf16[4,1024,192]{1,2,0:T(8,128)(2,1)}, u32[]{:S(2)}, u32[]{:S(2)}) %all-to-all-start.5) | async-done | bytes 1572896 | tf_op jit(solution)/shard_map/all_to_all | solution.py:252
  880.3 43.3 %all-reduce.1 = f32[11264]{0:T(1024)S(1)} all-reduce(f32[11264]{0:T(1024)S(1)} %constant_dynamic-update-slice_fusion), channel_id=3, replica_groups=mesh['rows'=8,'heads'=4] {'rows','heads'}, use_global_device_ids=true, to_apply=%region_30.31.clone | all-reduce | flops 11264 | bytes 90112
  924.3 294.3 %reduce-scatter.2.cloned.1.call-done = f32[480,768]{1,0:T(8,128)} async-done(((f32[15360,768]{1,0:T(8,128)}), f32[480,768]{1,0:T(8,128)}) %reduce-scatter.2.cloned.1.call-update) | async-done | bytes 1474576 | tf_op jit(solution)/shard_map/reduce_scatter | solution.py:300
  (286 shorter events, 342.9 us)
Async XLA Ops:
  7.2 51.9 %copy-start = (bf16[1024,768]{1,0:T(8,128)(2,1)S(1)}, bf16[1024,768]{1,0:T(8,128)(2,1)}, u32[]{:S(2)}) copy-start(bf16[1024,768]{1,0:T(8,128)(2,1)} %param.26) | copy-start | bytes 4718596
  7.2 173.5 %all-gather.2.cloned.1.call-start = ((), (), s32[]{:S(2)}) async-start(), calls=%async_computation.9 | async-start | bytes 24330240 | tf_op jit(solution)/shard_map/all_gather | solution.py:165
  64.2 25.0 %all-to-all-start.1 = ((bf16[1024,4,192]{0,2,1:T(8,128)(2,1)}), bf16[1024,4,192]{0,2,1:T(8,128)(2,1)S(1)}, u32[]{:S(2)}, u32[]{:S(2)}) async-start(bf16[1024,4,192]{0,2,1:T(8,128)(2,1)} %bitcast.193), calls=%async_computation.1 | async-start | bytes 3145728 | tf_op jit(solution)/shard_map/all_to_all | solution.py:192
  75.8 18.0 %copy-start.37 = (s32[640]{0:T(1024)S(1)}, s32[640]{0:T(1024)}, u32[]{:S(2)}) copy-start(s32[640]{0:T(1024)} %param.27) | copy-start | bytes 7684
  89.2 168.2 %all-to-all-start = ((bf16[1024,4,192]{0,2,1:T(8,128)(2,1)}), bf16[1024,4,192]{0,2,1:T(8,128)(2,1)}, u32[]{:S(2)}, u32[]{:S(2)}) async-start(bf16[1024,4,192]{0,2,1:T(8,128)(2,1)} %bitcast.191), calls=%async_computation | async-start | bytes 3145728 | tf_op jit(solution)/shard_map/all_to_all | solution.py:194
  257.4 24.9 %all-to-all-start.2 = ((bf16[1024,4,192]{0,2,1:T(8,128)(2,1)}), bf16[1024,4,192]{0,2,1:T(8,128)(2,1)}, u32[]{:S(2)}, u32[]{:S(2)}) async-start(bf16[1024,4,192]{0,2,1:T(8,128)(2,1)} %bitcast.192), calls=%async_computation.2 | async-start | bytes 3145728 | tf_op jit(solution)/shard_map/all_to_all | solution.py:193
  333.3 16.5 %copy-start.2 = (bf16[4,1024,3,64]{1,3,2,0:T(8,128)(2,1)}, bf16[4,1024,3,64]{1,3,2,0:T(8,128)(2,1)S(1)}, u32[]{:S(2)}) copy-start(bf16[4,1024,3,64]{1,3,2,0:T(8,128)(2,1)S(1)} %get-tuple-element.412) | copy-start | bytes 4718596
  333.3 16.5 %copy-start.29 = (pred[4,1024]{1,0:T(4,128)(4,1)}, pred[4,1024]{1,0:T(4,128)(4,1)S(1)}, u32[]{:S(2)}) copy-start(pred[4,1024]{1,0:T(4,128)(4,1)S(1)} %get-tuple-element.428) | copy-start | bytes 12292
  333.3 34.6 %all-to-all-start.3 = ((bf16[4,1024,192]{1,2,0:T(8,128)(2,1)}), bf16[4,1024,192]{1,2,0:T(8,128)(2,1)}, u32[]{:S(2)}, u32[]{:S(2)}) async-start(bf16[4,1024,192]{1,2,0:T(8,128)(2,1)} %bitcast.186), calls=%async_computation.3 | async-start | bytes 3145728 | tf_op jit(solution)/shard_map/all_to_all | solution.py:207
  368.0 39.9 %slice-start.2 = ((s8[4718592]{0:T(1024)(128)(4,1)}), s8[4194304]{0:T(1024)(128)(4,1)S(1)}, s32[]{:S(2)}) async-start(s8[4718592]{0:T(1024)(128)(4,1)} %bitcast.189), calls=%async_computation.13 | async-start | bytes 8388608
  371.6 76.1 %copy-start.9 = (f32[1024,768]{0,1:T(8,128)}, f32[1024,768]{0,1:T(8,128)S(1)}, u32[]{:S(2)}) copy-start(f32[1024,768]{0,1:T(8,128)S(1)} %get-tuple-element.227) | copy-start | bytes 9437188
  372.3 35.6 %slice-start.3 = ((s8[4718592]{0:T(1024)(128)(4,1)}), s8[524288]{0:T(1024)(128)(4,1)S(1)}, s32[]{:S(2)}) async-start(s8[4718592]{0:T(1024)(128)(4,1)} %bitcast.189), calls=%async_computation.14 | async-start | bytes 1048576
  372.3 35.6 %copy-start.53 = (f32[768]{0:T(1024)S(1)}, f32[768]{0:T(1024)}, u32[]{:S(2)}) copy-start(f32[768]{0:T(1024)} %get-tuple-element.215) | copy-start | bytes 9220
  453.9 24.5 %all-to-all-start.4 = ((bf16[1024,4,192]{0,2,1:T(8,128)(2,1)}), bf16[1024,4,192]{0,2,1:T(8,128)(2,1)}, u32[]{:S(2)}, u32[]{:S(2)}) async-start(bf16[1024,4,192]{0,2,1:T(8,128)(2,1)} %bitcast.35), calls=%async_computation.4 | async-start | bytes 3145728 | tf_op jit(solution)/shard_map/all_to_all | solution.py:240
  595.0 24.5 %all-to-all-start.6 = ((bf16[4,1024,192]{1,2,0:T(8,128)(2,1)}), bf16[4,1024,192]{1,2,0:T(8,128)(2,1)}, u32[]{:S(2)}, u32[]{:S(2)}) async-start(bf16[4,1024,192]{1,2,0:T(8,128)(2,1)} %bitcast.185), calls=%async_computation.6 | async-start | bytes 3145728 | tf_op jit(solution)/shard_map/all_to_all | solution.py:255
  599.4 20.1 %copy-start.23 = (bf16[1024,768]{1,0:T(8,128)(2,1)S(1)}, bf16[1024,768]{1,0:T(8,128)(2,1)}, u32[]{:S(2)}) copy-start(bf16[1024,768]{1,0:T(8,128)(2,1)} %param.19) | copy-start | bytes 4718596
  599.4 619.2 %reduce-scatter.2.cloned.1.call-start = ((), (), s32[]{:S(2)}) async-start(), calls=%async_computation.10 | async-start | bytes 48660480 | tf_op jit(solution)/shard_map/reduce_scatter | solution.py:300
  636.6 26.9 %copy-start.39 = (s32[2048]{0:T(1024)S(1)}, s32[2048]{0:T(1024)}, u32[]{:S(2)}) copy-start(s32[2048]{0:T(1024)} %pad_clamp_fusion) | copy-start | bytes 24580
  723.7 54.9 %copy-start.31 = (f32[15360]{0:T(1024)S(1)}, f32[15360]{0:T(1024)}, u32[]{:S(2)}) copy-start(f32[15360]{0:T(1024)} %mul.341) | copy-start | bytes 184324
  809.7 24.6 %all-to-all-start.5 = ((bf16[4,1024,192]{1,2,0:T(8,128)(2,1)}), bf16[4,1024,192]{1,2,0:T(8,128)(2,1)}, u32[]{:S(2)}, u32[]{:S(2)}) async-start(bf16[4,1024,192]{1,2,0:T(8,128)(2,1)} %bitcast.39), calls=%async_computation.5 | async-start | bytes 3145728 | tf_op jit(solution)/shard_map/all_to_all | solution.py:252
  834.3 23.9 %all-to-all-start.7 = ((bf16[4,1024,192]{1,2,0:T(8,128)(2,1)}), bf16[4,1024,192]{1,2,0:T(8,128)(2,1)S(1)}, u32[]{:S(2)}, u32[]{:S(2)}) async-start(bf16[4,1024,192]{1,2,0:T(8,128)(2,1)} %bitcast.45), calls=%async_computation.7 | async-start | bytes 3145728 | tf_op jit(solution)/shard_map/all_to_all | solution.py:258
  879.3 44.3 %copy-start.49 = (f32[352]{0:T(512)S(1)}, f32[352]{0:T(512)}, u32[]{:S(2)}) copy-start(f32[352]{0:T(512)} %param.31) | copy-start | bytes 4228
  879.3 44.3 %copy-start.58 = (f32[352]{0:T(512)S(1)}, f32[352]{0:T(512)}, u32[]{:S(2)}) copy-start(f32[352]{0:T(512)} %param.32) | copy-start | bytes 4228
  879.3 44.3 %copy-start.59 = (f32[352]{0:T(512)S(1)}, f32[352]{0:T(512)}, u32[]{:S(2)}) copy-start(f32[352]{0:T(512)} %param.33) | copy-start | bytes 4228
  (56 other events, 284.8 us)
Sparse Core Ops, SparseCore 0:
  11.5 169.1 all-gather.1
  809.8 408.7 reduce-scatter.1
where the time goes:
time: 1240 us; the launch traced here: 1230 us
  waiting for transfers between devices  442 us (36%)
  local copies, waits for them, and re-layouts  275 us (22%)
  matrix products  270 us (22%)
  other arithmetic  107 us (9%)
  blocking collectives  87.4 us (7%)
  starting transfers between devices  34.6 us (3%)
  between operations  15.3 us (1%)
    reduce_scatter x1, waiting for transfers between devices, body(): lax.psum_scatter(slotted, ('rows', 'heads'), scatter_dimension=0, tiled=T...  294 us
    gather x2, local copies, waits for them, and re-layouts, body(): grad_rows[source] * filled.astype(jnp.float32)[:, None, None]  115 us
    unnamed x2, blocking collectives  87.4 us
    all_gather x1, waiting for transfers between devices, body(): lax.all_gather(weights.astype(jnp.bfloat16), ('rows', 'heads'), axis=0, t...  86.6 us
    dot_general x9, matrix products, product_t(): lax.dot_general(left, right, (((1,), (1,)), ((), ())), preferred_element_...  80.3 us
    dot_general x9, matrix products, product(): return jnp.dot(left, right, preferred_element_type=jnp.float32)  40.6 us
    reshape x1, local copies, waits for them, and re-layouts, unpack_rows(): rows = gathered.reshape(-1, BLOCK_ROWS, D)[slot].reshape(-1, D)  36.1 us
    slice x6, local copies, waits for them, and re-layouts, unpack_rows(): return (rows[:D], rows[D:2 * D], rows[2 * D:2 * D + FF], rows[2 * D + FF:])  35.4 us
  transfers between devices with their start and end apart: 10, of which 8 were waited for; matrix products, arithmetic and copies ran while one was open for 16% of the time, Pallas kernels for 0%

commit v1 on v0

v1 whole, which is shorter than its diff:
```python
import jax
import jax.numpy as jnp
from jax import lax
from jax.experimental import pallas as pl
from jax.experimental.pallas import tpu as pltpu
from jax.sharding import PartitionSpec as P

D = 768
FF = 3072
HEAD_DIM = 64
RANK = 1024
SEQ_LEN = 1024
STEP = 3
BLOCK_ROWS = 12


def slot_index(owner, capacity):
    count = owner.shape[0]
    order = jnp.arange(count, dtype=jnp.int32)
    same_owner = owner[:, None] == owner[None, :]
    earlier = order[None, :] < order[:, None]
    ranked = jnp.sum((same_owner & earlier).astype(jnp.int32), axis=1)
    return owner * capacity + ranked


def split_small(vector):
    widths = [RANK, RANK, D, D, D, FF, D, D, D, D, D]
    pieces = []
    offset = 0
    for width in widths:
        pieces.append(vector[offset : offset + width])
        offset = offset + width
    return pieces


def unpack_rows(gathered, slot):
    rows = gathered.reshape(-1, BLOCK_ROWS, D)[slot].reshape(-1, D)
    return (rows[:D], rows[D : 2 * D], rows[2 * D : 2 * D + FF], rows[2 * D + FF :])


def product(left, right):
    return jnp.dot(left, right, preferred_element_type=jnp.float32)


def product_t(left, right):
    return lax.dot_general(
        left, right, (((1,), (1,)), ((), ())), preferred_element_type=jnp.float32
    )


def inner_rows(left, right):
    return lax.dot_general(
        left, right, (((0,), (0,)), ((), ())), preferred_element_type=jnp.float32
    )


def normalize(values):
    centre = jnp.mean(values, axis=-1, keepdims=True)
    centred = values - centre
    spread = jnp.mean(centred * centred, axis=-1, keepdims=True)
    inverse = lax.rsqrt(spread + 1e-05)
    return (centred * inverse, inverse)


def norm_back(grad_norm, normed, inverse):
    first_mean = jnp.mean(grad_norm, axis=-1, keepdims=True)
    second_mean = jnp.mean(grad_norm * normed, axis=-1, keepdims=True)
    return inverse * (grad_norm - first_mean - normed * second_mean)


PAIR = 2 * HEAD_DIM
TILE = 256


def lane_split(rows):
    return lax.broadcasted_iota(jnp.int32, (rows, PAIR), 1)


def visible_bias(spans, rows):
    place = lax.broadcasted_iota(jnp.int32, (rows, PAIR), 0)
    first_end = spans[0]
    begin = spans[2]
    seen = (place < first_end) | ((place >= begin) & (place < begin + spans[1]))
    return jnp.where(seen, 0.0, -1e30)


def score_operands(query, keys, bias, lanes, half):
    mine = (lanes < HEAD_DIM) == (half == 0)
    spare = lanes == (HEAD_DIM if half == 0 else 0)
    query_h = jnp.where(mine, query * 0.125, jnp.where(spare, 1.0, 0.0)).astype(jnp.bfloat16)
    keys_h = jnp.where(mine, keys, bias).astype(jnp.bfloat16)
    return (mine, query_h, keys_h)


def attend_forward_kernel(spans, query_ref, keys_ref, values_ref, context_ref, total_ref, turned):
    rows = query_ref.shape[0]
    lanes = lane_split(rows)
    bias = visible_bias(spans, rows)
    query = query_ref[...].astype(jnp.float32)
    keys = keys_ref[...].astype(jnp.float32)
    values_t = values_ref[...].astype(jnp.float32).T
    feature = lax.broadcasted_iota(jnp.int32, values_t.shape, 0)
    for half in range(2):
        _, query_h, keys_h = score_operands(query, keys, bias, lanes, half)
        own = (feature < HEAD_DIM) == (half == 0)
        values_h = jnp.where(own, values_t, 1.0).astype(jnp.bfloat16)
        low = half * HEAD_DIM
        other = HEAD_DIM - low
        for start in range(0, rows, TILE):
            scores = product_t(keys_h, query_h[start : start + TILE])
            highest = jnp.max(scores, axis=0, keepdims=True)
            raised = jnp.exp(scores - highest).astype(jnp.bfloat16)
            mixed = product(values_h, raised)
            summed = mixed[other : other + 1]
            total_ref[0, half : half + 1, start : start + TILE] = highest + jnp.log(summed)
            turned[low : low + HEAD_DIM, start : start + TILE] = (
                mixed[low : low + HEAD_DIM] / summed
            )
    context_ref[...] = turned[...].T.astype(jnp.bfloat16)


def attend_backward_kernel(
    spans,
    query_ref,
    keys_ref,
    values_ref,
    context_ref,
    grad_ref,
    total_ref,
    grad_query_ref,
    grad_keys_ref,
    grad_values_ref,
    turned,
    keys_sum,
    values_sum,
):
    rows = query_ref.shape[0]
    lanes = lane_split(rows)
    bias = visible_bias(spans, rows)
    query = query_ref[...].astype(jnp.float32)
    keys = keys_ref[...].astype(jnp.float32)
    values = values_ref[...].astype(jnp.float32)
    grad = grad_ref[...].astype(jnp.float32)
    dots = (grad * context_ref[...].astype(jnp.float32)).T
    keys_t = keys.T
    feature = lax.broadcasted_iota(jnp.int32, keys_t.shape, 0)
    grad_low = grad_ref[...]
    for half in range(2):
        mine, query_h, keys_h = score_operands(query, keys, bias, lanes, half)
        values_h = jnp.where(mine, values, 0.0).astype(jnp.bfloat16)
        grad_h = jnp.where(mine, grad, 0.0).astype(jnp.bfloat16)
        query_m = jnp.where(mine, query * 0.125, 0.0).astype(jnp.bfloat16)
        own = (feature < HEAD_DIM) == (half == 0)
        keys_th = jnp.where(own, keys_t * 0.125, 0.0).astype(jnp.bfloat16)
        low = half * HEAD_DIM
        row_dot = jnp.sum(dots[low : low + HEAD_DIM], axis=0, keepdims=True)
        for start in range(0, rows, TILE):
            part = slice(start, start + TILE)
            scores = product_t(keys_h, query_h[part])
            probs = jnp.exp(scores - total_ref[0, half : half + 1, part])
            grad_probs = product_t(values_h, grad_low[part])
            grad_scores = (probs * (grad_probs - row_dot[:, part])).astype(jnp.bfloat16)
            values_part = product(probs.astype(jnp.bfloat16), grad_h[part])
            keys_part = product(grad_scores, query_m[part])
            query_part = product(keys_th, grad_scores)
            if half == 0 and start == 0:
                values_sum[...] = values_part
                keys_sum[...] = keys_part
            else:
                values_sum[...] += values_part
                keys_sum[...] += keys_part
            if half == 0:
                turned[:, part] = query_part
            else:
                turned[:, part] += query_part
    grad_query_ref[...] = turned[...].T.astype(jnp.bfloat16)
    grad_keys_ref[...] = keys_sum[...].astype(jnp.bfloat16)
    grad_values_ref[...] = values_sum[...].astype(jnp.bfloat16)


def pair_specs(rows):
    wide = pl.BlockSpec((rows, PAIR), lambda i, spans: (0, i))
    total = pl.BlockSpec((1, 2, rows), lambda i, spans: (i, 0, 0))
    return (wide, total)


def attend_forward(spans, query, keys, values):
    rows, width = query.shape
    pairs = width // PAIR
    wide, total = pair_specs(rows)
    return pl.pallas_call(
        attend_forward_kernel,
        out_shape=(
            jax.ShapeDtypeStruct((rows, width), jnp.bfloat16),
            jax.ShapeDtypeStruct((pairs, 2, rows), jnp.float32),
        ),
        grid_spec=pltpu.PrefetchScalarGridSpec(
            num_scalar_prefetch=1,
            grid=(pairs,),
            in_specs=[wide, wide, wide],
            out_specs=(wide, total),
            scratch_shapes=[pltpu.VMEM((PAIR, rows), jnp.float32)],
        ),
        name="attend_forward",
    )(spans, query, keys, values)


def attend_backward(spans, query, keys, values, context, grad_context, log_total):
    rows, width = query.shape
    pairs = width // PAIR
    wide, total = pair_specs(rows)
    shape = jax.ShapeDtypeStruct((rows, width), jnp.bfloat16)
    return pl.pallas_call(
        attend_backward_kernel,
        out_shape=(shape, shape, shape),
        grid_spec=pltpu.PrefetchScalarGridSpec(
            num_scalar_prefetch=1,
            grid=(pairs,),
            in_specs=[wide, wide, wide, wide, wide, total],
            out_specs=(wide, wide, wide),
            scratch_shapes=[
                pltpu.VMEM((PAIR, rows), jnp.float32),
                pltpu.VMEM((rows, PAIR), jnp.float32),
                pltpu.VMEM((rows, PAIR), jnp.float32),
            ],
        ),
        name="attend_backward",
    )(spans, query, keys, values, context, grad_context, log_total)


AXES = ("rows", "heads")


def exchange(values, bit, devices):
    return lax.ppermute(values, AXES, [(i, i ^ bit) for i in range(devices)])


def my_bit(bit):
    return (lax.axis_index(AXES) & bit) != 0


def gather_small(values, devices):
    rows = values[None, :]
    bit = 1
    while bit < devices:
        other = exchange(rows, bit, devices)
        rows = jnp.where(
            my_bit(bit),
            jnp.concatenate([other, rows], axis=0),
            jnp.concatenate([rows, other], axis=0),
        )
        bit = bit * 2
    return rows.reshape(-1)


def reduce_halves(values, devices):
    bit = 1
    while bit < devices:
        half = values.shape[0] // 2
        upper = my_bit(bit)
        low_part = values[:half]
        high_part = values[half:]
        keep = jnp.where(upper, high_part, low_part).astype(jnp.float32)
        sent = jnp.where(upper, low_part, high_part)
        values = (keep + exchange(sent, bit, devices).astype(jnp.float32)).astype(values.dtype)
        bit = bit * 2
    return values


def reverse_bits(count):
    width = count.bit_length() - 1
    return [int(format(i, "b").zfill(width)[::-1], 2) for i in range(count)]


def all_to_all(values):
    return lax.all_to_all(values, AXES, split_axis=0, concat_axis=0, tiled=True)


def pieces_of(rows, devices):
    return rows.reshape(-1, devices, BLOCK_ROWS * D // devices).transpose(1, 0, 2)


def rows_of(pieces):
    return pieces.transpose(1, 0, 2).reshape(-1, D)


def route_in(rows, place, slots, devices):
    pieces = all_to_all(pieces_of(rows, devices)).reshape(slots, -1)
    chosen = place[:, None] == jnp.arange(slots, dtype=jnp.int32)[None, :]
    homed = product(chosen.astype(jnp.bfloat16), pieces).astype(jnp.bfloat16)
    return rows_of(all_to_all(homed.reshape(devices, -1, pieces.shape[1])))


def route_out(rows, place, slots, devices):
    pieces = all_to_all(pieces_of(rows, devices)).reshape(place.shape[0], -1)
    chosen = place[:, None] == jnp.arange(slots, dtype=jnp.int32)[None, :]
    slotted = inner_rows(chosen.astype(jnp.bfloat16), pieces).astype(jnp.bfloat16)
    return rows_of(all_to_all(slotted.reshape(devices, -1, pieces.shape[1])))


def gather_rows(weights, slot, devices):
    blocks = slot.shape[0]
    slots = devices * (weights.shape[0] // BLOCK_ROWS)
    low = weights.astype(jnp.bfloat16)
    if blocks % devices == 0 and (BLOCK_ROWS * D) % devices == 0:
        homed = route_in(low, slot, slots, devices)
        rows = lax.all_gather(homed, AXES, axis=0, tiled=True)
        return (rows[:D], rows[D : 2 * D], rows[2 * D : 2 * D + FF], rows[2 * D + FF :])
    return unpack_rows(lax.all_gather(low, AXES, axis=0, tiled=True), slot)


def scatter_grads(grad_key, grad_rest, small_grad, slot, slots, devices):
    key_blocks = D // BLOCK_ROWS
    blocks = slot.shape[0]
    share = small_grad.shape[0] // devices
    if key_blocks % devices or (blocks - key_blocks) % devices or share > D:
        rows = jnp.concatenate([grad_key, *grad_rest], axis=0).reshape(blocks, BLOCK_ROWS * D)
        chosen = slot[:, None] == jnp.arange(slots, dtype=jnp.int32)[None, :]
        slotted = inner_rows(chosen.astype(jnp.bfloat16), rows).astype(jnp.bfloat16)
        return (
            lax.psum_scatter(slotted.reshape(-1, D), AXES, scatter_dimension=0, tiled=True),
            lax.psum_scatter(small_grad, AXES, scatter_dimension=0, tiled=True),
        )
    rest = jnp.concatenate(grad_rest, axis=0)
    rest_home = lax.psum_scatter(rest, AXES, scatter_dimension=0, tiled=True)
    order = jnp.array(reverse_bits(devices), dtype=jnp.int32)
    key_rows = D // devices
    wide = -(-(key_rows + 1) // 16) * 16
    small_rows = small_grad.reshape(devices, share)[order].astype(jnp.bfloat16)
    small_rows = jnp.pad(small_rows[:, None, :], ((0, 0), (0, wide - key_rows - 1), (0, D - share)))
    packed = jnp.concatenate([grad_key.reshape(devices, key_rows, D), small_rows], axis=1)
    summed = reduce_halves(packed.reshape(-1, D), devices)
    home = jnp.concatenate([summed[:key_rows], rest_home], axis=0)
    place = jnp.concatenate(
        [
            slot[:key_blocks].reshape(devices, -1)[order],
            slot[key_blocks:].reshape(devices, -1),
        ],
        axis=1,
    ).reshape(-1)
    return (
        route_out(home, place, slots, devices).astype(jnp.float32),
        summed[key_rows, :share].astype(jnp.float32),
    )


def adamw_update(master, first, second, grad, decay, rate):
    correct = 1.0 - 0.5**STEP
    first_new = 0.5 * first + 0.5 * grad
    second_new = 0.5 * second + 0.5 * grad * grad
    update = first_new / correct / (jnp.sqrt(second_new / correct) + 1e-08) + decay * master
    return (master - rate * update, first_new, second_new)


def body(
    hidden_in,
    cotangent,
    part_lengths,
    segment_start,
    query_weight,
    value_weight,
    shared_down,
    shared_up,
    owner,
    weights,
    first_moment,
    second_moment,
    small_weights,
    small_first,
    small_second,
):
    capacity = weights.shape[0] // BLOCK_ROWS
    devices = lax.axis_size("rows") * lax.axis_size("heads")
    slot = slot_index(owner, capacity)
    small_all = gather_small(small_weights.astype(jnp.bfloat16), devices)
    key_rows, out_rows, up_rows, down_rows = gather_rows(weights, slot, devices)
    (
        scale_q_rank,
        scale_v_rank,
        scale_q_out,
        scale_v_out,
        out_bias,
        up_bias,
        down_bias,
        gain_one,
        shift_one,
        gain_two,
        shift_two,
    ) = [piece.astype(jnp.float32) for piece in split_small(small_all)]
    projected = product(hidden_in, shared_down).astype(jnp.bfloat16)
    projected_wide = projected.astype(jnp.float32)
    rank_q = (scale_q_rank * projected_wide).astype(jnp.bfloat16)
    rank_v = (scale_v_rank * projected_wide).astype(jnp.bfloat16)
    side_q = product(rank_q, shared_up)
    side_v = product(rank_v, shared_up)
    query = (product(hidden_in, query_weight) + scale_q_out * side_q).astype(jnp.bfloat16)
    keys = product(hidden_in, key_rows).astype(jnp.bfloat16)
    values = (product(hidden_in, value_weight) + scale_v_out * side_v).astype(jnp.bfloat16)
    mine = lax.axis_index("heads")
    spans = jnp.concatenate([part_lengths[mine], segment_start[mine][None]])
    context, log_total = attend_forward(spans, query, keys, values)
    attended = product(context, out_rows) + out_bias
    first_sum = hidden_in.astype(jnp.float32) + attended
    norm_one, inverse_one = normalize(first_sum)
    hidden_one = norm_one * gain_one + shift_one
    hidden_low = hidden_one.astype(jnp.bfloat16)
    pre_act = product_t(hidden_low, up_rows) + up_bias
    share = 0.5 * (1.0 + lax.erf(pre_act * 0.7071067811865476))
    slope = share + pre_act * jnp.exp(-0.5 * pre_act * pre_act) * 0.3989422804014327
    active, slope = lax.optimization_barrier(
        ((pre_act * share).astype(jnp.bfloat16), slope.astype(jnp.bfloat16))
    )
    second_sum = hidden_one + product(active, down_rows) + down_bias
    norm_two, inverse_two = normalize(second_sum)
    block_out = (norm_two * gain_two + shift_two).astype(jnp.bfloat16)
    grad_top = cotangent.astype(jnp.float32)
    grad_gain_two = jnp.sum(grad_top * norm_two, axis=0)
    grad_shift_two = jnp.sum(grad_top, axis=0)
    grad_second = norm_back(grad_top * gain_two, norm_two, inverse_two)
    grad_branch = grad_second.astype(jnp.bfloat16)
    grad_down_bias = jnp.sum(grad_branch.astype(jnp.float32), axis=0)
    grad_down = inner_rows(active, grad_branch).astype(jnp.bfloat16)
    grad_pre = (product_t(grad_branch, down_rows) * slope.astype(jnp.float32)).astype(jnp.bfloat16)
    grad_up_bias = jnp.sum(grad_pre.astype(jnp.float32), axis=0)
    grad_up = inner_rows(grad_pre, hidden_low).astype(jnp.bfloat16)
    grad_hidden = grad_second + product(grad_pre, up_rows)
    grad_gain_one = jnp.sum(grad_hidden * norm_one, axis=0)
    grad_shift_one = jnp.sum(grad_hidden, axis=0)
    grad_first = norm_back(grad_hidden * gain_one, norm_one, inverse_one)
    grad_attended = grad_first.astype(jnp.bfloat16)
    grad_out_bias = jnp.sum(grad_attended.astype(jnp.float32), axis=0)
    grad_out = inner_rows(context, grad_attended).astype(jnp.bfloat16)
    grad_context = product_t(grad_attended, out_rows).astype(jnp.bfloat16)
    grad_query, grad_keys, grad_values = attend_backward(
        spans, query, keys, values, context, grad_context, log_total
    )
    grad_key = inner_rows(hidden_in, grad_keys).astype(jnp.bfloat16)
    grad_query_wide = grad_query.astype(jnp.float32)
    grad_values_wide = grad_values.astype(jnp.float32)
    grad_scale_q_out = jnp.sum(grad_query_wide * side_q, axis=0)
    grad_scale_v_out = jnp.sum(grad_values_wide * side_v, axis=0)
    grad_side_q = (scale_q_out * grad_query_wide).astype(jnp.bfloat16)
    grad_side_v = (scale_v_out * grad_values_wide).astype(jnp.bfloat16)
    grad_rank_q = product_t(grad_side_q, shared_up)
    grad_rank_v = product_t(grad_side_v, shared_up)
    grad_scale_q_rank = jnp.sum(grad_rank_q * projected_wide, axis=0)
    grad_scale_v_rank = jnp.sum(grad_rank_v * projected_wide, axis=0)
    grad_projected = (grad_rank_q * scale_q_rank + grad_rank_v * scale_v_rank).astype(jnp.bfloat16)
    grad_input = grad_first + product_t(grad_query, query_weight) + product_t(grad_keys, key_rows)
    grad_input = (
        grad_input + product_t(grad_values, value_weight) + product_t(grad_projected, shared_down)
    )
    input_grad = grad_input.astype(jnp.bfloat16)
    small_grad = jnp.concatenate(
        [
            grad_scale_q_rank,
            grad_scale_v_rank,
            grad_scale_q_out,
            grad_scale_v_out,
            grad_out_bias,
            grad_up_bias,
            grad_down_bias,
            grad_gain_one,
            grad_shift_one,
            grad_gain_two,
            grad_shift_two,
        ]
    )
    owned_grad, owned_small = scatter_grads(
        grad_key, (grad_out, grad_up, grad_down), small_grad, slot, devices * capacity, devices
    )
    new_weights, new_first, new_second = adamw_update(
        weights, first_moment, second_moment, owned_grad, 0.01, 0.03
    )
    new_small, new_small_first, new_small_second = adamw_update(
        small_weights, small_first, small_second, owned_small, 0.0, 0.3
    )
    return (
        block_out,
        input_grad,
        new_weights,
        new_first,
        new_second,
        new_weights.astype(jnp.bfloat16),
        new_small,
        new_small_first,
        new_small_second,
        new_small.astype(jnp.bfloat16),
    )


def solution(mesh):
    return jax.shard_map(
        body,
        mesh=mesh,
        in_specs=(
            P(("rows", "heads"), None),
            P(("rows", "heads"), None),
            P("rows", None),
            P("rows"),
            P(),
            P(),
            P(),
            P(),
            P(),
            P(("rows", "heads"), None),
            P(("rows", "heads"), None),
            P(("rows", "heads"), None),
            P(("rows", "heads")),
            P(("rows", "heads")),
            P(("rows", "heads")),
        ),
        out_specs=(
            P(("rows", "heads"), None),
            P(("rows", "heads"), None),
            P(("rows", "heads"), None),
            P(("rows", "heads"), None),
            P(("rows", "heads"), None),
            P(("rows", "heads"), None),
            P(("rows", "heads")),
            P(("rows", "heads")),
            P(("rows", "heads")),
            P(("rows", "heads")),
        ),
        check_vma=False,
    )
```

time: 1240 us -> 522 us (0.42)
  waiting for transfers between devices: 442 us -> 175 us
  local copies, waits for them, and re-layouts: 275 us -> 32.9 us
  matrix products: 270 us -> 126 us
  Pallas kernels: 0 us -> 72.5 us
  blocking collectives: 87.4 us -> 20.2 us
  other arithmetic: 107 us -> 45.6 us
    reduce_scatter x1, waiting for transfers between devices: 294 us -> 51.5 us  [scatter_grads(): rest_home = lax.psum_scatter(rest, AXES, scatter_dimension=0, tiled=True)]
    gather x3 -> x2, local copies, waits for them, and re-layouts: 145 us -> 1.21 us  [the longest x1 0.63 us: scatter_grads(): small_rows = small_grad.reshape(devices, share)[order].astype(jnp.bfloat16)]
    dot_general x28 -> x0, matrix products: 121 us -> none  [the longest x8 25.8 us: masked_scores(): jnp.einsum('qhd,khd->hqk', query, keys, preferred_element_type=jnp.float32)]
    unnamed x2 -> x0, blocking collectives: 87.4 us -> none
    pallas_call x0 -> x2, Pallas kernels: none -> 72.5 us  [the longest x1 37.9 us: attend_forward(): pl.pallas_call(attend_forward_kernel, out_shape=(jax.ShapeDtypeStruct((ro...]
    reshape x2 -> x9, local copies, waits for them, and re-layouts: 63 us -> 10.9 us  [the longest x4 6.36 us: pieces_of(): rows.reshape(-1, devices, BLOCK_ROWS * D // devices).transpose(1, 0, 2)]
    slice x6 -> x4, local copies, waits for them, and re-layouts: 35.4 us -> 0.17 us  [the longest x2 0.09 us: scatter_grads(): slot[:key_blocks].reshape(devices, -1)[order]]
    mul x1 -> x0, other arithmetic: 31.1 us -> none  [body(): grad_rows[source] * filled.astype(jnp.float32)[:, None, None]]
  transfers between devices with their start and end apart: 10 -> 15, of which waited for: 8 -> 13; matrix products, arithmetic and copies ran while one was open for 16% -> 14% of each run, Pallas kernels for 0% -> 7%
where the time goes in v1:
time: 522 us; the launch traced here: 516 us
  waiting for transfers between devices  175 us (34%)
  matrix products  126 us (24%)
  Pallas kernels  72.5 us (14%)
  other arithmetic  45.6 us (9%)
  local copies, waits for them, and re-layouts  32.9 us (6%)
  starting transfers between devices  28.5 us (5%)
  blocking collectives  20.2 us (4%)
  between operations  15.1 us (3%)
    all_gather x1, waiting for transfers between devices, gather_rows(): rows = lax.all_gather(homed, AXES, axis=0, tiled=True)  57.4 us
    dot_general x9, matrix products, product_t(): lax.dot_general(left, right, (((1,), (1,)), ((), ())), preferred_element_...  56.1 us
    reduce_scatter x1, waiting for transfers between devices, scatter_grads(): rest_home = lax.psum_scatter(rest, AXES, scatter_dimension=0, tiled=True)  51.5 us
    dot_general x10, matrix products, product(): return jnp.dot(left, right, preferred_element_type=jnp.float32)  46 us
    all_to_all x3, waiting for transfers between devices, all_to_all(): return lax.all_to_all(values, AXES, split_axis=0, concat_axis=0, tiled=True)  38.5 us
    pallas_call x1, Pallas kernels, attend_forward(): pl.pallas_call(attend_forward_kernel, out_shape=(jax.ShapeDtypeStruct((ro...  37.9 us
    pallas_call x1, Pallas kernels, attend_backward(): pl.pallas_call(attend_backward_kernel, out_shape=(shape, shape, shape), g...  34.6 us
    ppermute x10, waiting for transfers between devices, exchange(): return lax.ppermute(values, AXES, [(i, i ^ bit) for i in range(devices)])  28.1 us
  transfers between devices with their start and end apart: 15, of which 13 were waited for; matrix products, arithmetic and copies ran while one was open for 14% of the time, Pallas kernels for 7%

profile of v1, /device:TPU:0, one launch (start us, length us, event | category | flops | bytes accessed | tf_op | source)
XLA Modules:
  0.0 515.9 jit_solution(11144100684405043188)
XLA Ops:
  11.6 7.3 %all-to-all-start = ((bf16[32,40,288]{2,1,0:T(8,128)(2,1)}), bf16[32,40,288]{2,1,0:T(8,128)(2,1)S(1)}, u32[]{:S(2)}, u32[]{:S(2)}) async-start(bf16[32,40,288]{2,1,0:T(8,128)(2,1)} %bitcast.50), calls=%async_computation | async-start | bytes 1966080 | tf_op jit(solution)/shard_map/all_to_all | solution.py:276
  19.3 24.4 %all-to-all-done = bf16[32,40,288]{2,1,0:T(8,128)(2,1)S(1)} async-done(((bf16[32,40,288]{2,1,0:T(8,128)(2,1)}), bf16[32,40,288]{2,1,0:T(8,128)(2,1)S(1)}, u32[]{:S(2)}, u32[]{:S(2)}) %all-to-all-start) | async-done | bytes 737312 | tf_op jit(solution)/shard_map/all_to_all | solution.py:276
  45.2 20.2 %all_to_all.20 = bf16[32,20,288]{2,1,0:T(8,128)(2,1)S(1)} all-to-all(bf16[32,20,288]{2,1,0:T(8,128)(2,1)S(1)} %reshape.143), channel_id=1, replica_groups=mesh['rows'=8,'heads'=4] {'rows','heads'}, dimensions={0} | all-to-all | bytes 737280 | tf_op jit(solution)/shard_map/all_to_all | solution.py:276
  77.2 5.0 convolution_convert_fusion.2
  100.4 57.4 %all-gather.2.cloned.1.call-done = bf16[7680,768]{1,0:T(8,128)(2,1)} async-done(((bf16[240,768]{1,0:T(8,128)(2,1)}), bf16[7680,768]{1,0:T(8,128)(2,1)}) %all-gather.2.cloned.1.call-update) | async-done | bytes 11796496 | tf_op jit(solution)/shard_map/all_gather | solution.py:307
  157.9 4.3 fusion.57.keys_ref
  162.1 37.9 %attend_forward.1 = (bf16[1024,768]{1,0:T(8,128)(2,1)}, f32[6,2,1024]{2,1,0:T(2,128)}) custom-call(s32[3]{0:T(128)} %pad_add_fusion.1.spans, bf16[1024,768]{1,0:T(8,128)(2,1)} %add_convert_fusion.4.query_ref, bf16[1024,768]{1,0:T(8,128)(2,1)} %fusion.57.keys_ref, bf16[1024,768]{1,0:T(8,128)(2,1)} %add_convert_fusion.3.values_ref), custom_call_target="tpu_custom_call" | custom-call | tf_op jit(solution)/shard_map/attend_forward/pallas_call | solution.py:191
  204.3 14.1 %fusion.4 = (bf16[1024,3072]{1,0:T(8,128)(2,1)}, bf16[1024,3072]{1,0:T(8,128)(2,1)S(1)}) fusion(f32[3072]{0:T(1024)S(1)} %slice_convert_fusion, bf16[7680,768]{1,0:T(8,128)(2,1)} %all-gather.2.cloned.1.call-done, f32[1024,768]{0,1:T(8,128)S(1)} %get-tuple-element.102, f32[768]{0:T(1024)S(1)} %get-tuple-element.94, f32[768]{0:T(1024)S(1)} %get-tuple-element.95, ...), kind=kOutput, calls=%fused_computation.7 | convolution fusion | flops 4873519104 | bytes 20473856 | tf_op jit(solution)/shard_map/dot_general | solution.py:46
  218.4 9.4 %fusion.78 = (f32[1024]{0:T(1024)S(1)}, f32[1024,768]{0,1:T(8,128)S(1)}) fusion(f32[768]{0:T(1024)S(1)} %get-tuple-element.93, bf16[1024,3072]{1,0:T(8,128)(2,1)S(1)} %get-tuple-element.18, bf16[7680,768]{1,0:T(8,128)(2,1)} %all-gather.2.cloned.1.call-done, f32[768]{0:T(1024)S(1)} %get-tuple-element.94, f32[768]{0:T(1024)S(1)} %get-tuple-element.95, ...), kind=kOutput, calls=%fused_computation.177 | convolution fusion | flops 4837342208 | bytes 17323008 | tf_op jit(solution)/shard_map/dot_general | solution.py:42
  232.5 5.5 %convolution_convert_fusion = bf16[3072,768]{1,0:T(8,128)(2,1)S(1)} fusion(bf16[1024,3072]{1,0:T(8,128)(2,1)S(1)} %bitcast.64, bf16[1024,768]{0,1:T(8,128)(2,1)S(1)} %get-tuple-element.83), kind=kOutput, calls=%fused_computation.17 | convolution fusion | flops 4834197504 | bytes 12582912 | tf_op jit(solution)/shard_map/dot_general | solution.py:52
  238.0 9.4 %convert_reduce_fusion = (f32[3072]{0:T(1024)S(1)}, bf16[1024,3072]{1,0:T(8,128)(2,1)}) fusion(bf16[1024,3072]{1,0:T(8,128)(2,1)S(1)} %bitcast.62, bf16[1024,768]{0,1:T(8,128)(2,1)S(1)} %get-tuple-element.83, bf16[7680,768]{1,0:T(8,128)(2,1)} %all-gather.2.cloned.1.call-done), kind=kOutput, calls=%fused_computation.8 | convolution fusion | flops 4847563776 | bytes 18886656 | tf_op jit(solution)/shard_map/dot_general | solution.py:46
  247.4 10.2 %convolution_convert_fusion.1 = bf16[3072,768]{1,0:T(8,128)(2,1)} fusion(bf16[1024,3072]{1,0:T(8,128)(2,1)} %get-tuple-element.108, f32[1024,768]{0,1:T(8,128)S(1)} %get-tuple-element.102, f32[768]{0:T(1024)S(1)} %get-tuple-element.94, f32[768]{0:T(1024)S(1)} %get-tuple-element.95, f32[1024]{0:T(1024)S(1)} %add_rsqrt_fusion.1, ...), kind=kOutput, calls=%fused_computation.18 | convolution fusion | flops 4838129664 | bytes 14170112 | tf_op jit(solution)/shard_map/dot_general | solution.py:52
  257.6 12.0 %multiply_reduce_fusion = (f32[768]{0:T(1024)S(1)}, f32[1024]{0:T(1024)S(1)}, f32[1024]{0:T(1024)S(1)}, f32[768]{0:T(1024)S(1)}, f32[1024,768]{0,1:T(8,128)}) fusion(f32[1024,768]{0,1:T(8,128)S(1)} %get-tuple-element.102, f32[1024]{0:T(1024)S(1)} %add_rsqrt_fusion.1, f32[1024]{0:T(1024)S(1)} %broadcast_multiply_fusion.5, f32[768]{0:T(1024)S(1)} %get-tuple-element.95, ...), kind=kOutput, calls=%fused_computation.54 | convolution fusion | flops 4845989888 | bytes 22065152 | tf_op jit(solution)/shard_map/dot_general | solution.py:42
  274.4 21.4 %pad_maximum_fusion = bf16[6912,768]{1,0:T(8,128)(2,1)} fusion(bf16[3072,768]{1,0:T(8,128)(2,1)S(1)} %convolution_convert_fusion, bf16[3072,768]{1,0:T(8,128)(2,1)S(1)} %bitcast.53, bf16[768,768]{1,0:T(8,128)(2,1)S(1)} %convolution_convert_fusion.5), kind=kLoop, calls=%fused_computation.12 | loop fusion | flops 31850496 | bytes 21233664 | tf_op jit(solution)/shard_map/concatenate | solution.py:324
  296.5 4.8 convolution_convert_fusion.4.grad_ref
  301.3 34.6 %attend_backward.1 = (bf16[1024,768]{1,0:T(8,128)(2,1)}, bf16[1024,768]{1,0:T(8,128)(2,1)}, bf16[1024,768]{1,0:T(8,128)(2,1)}) custom-call(s32[3]{0:T(128)} %pad_add_fusion.1.spans, bf16[1024,768]{1,0:T(8,128)(2,1)} %add_convert_fusion.4.query_ref, bf16[1024,768]{1,0:T(8,128)(2,1)} %fusion.57.keys_ref, bf16[1024,768]{1,0:T(8,128)(2,1)} %add_convert_fusion.3.values_ref, ...), custom_call_target="tpu_custom_call" | custom-call | tf_op jit(solution)/shard_map/attend_backward/pallas_call | solution.py:213
  355.5 11.6 %collective-permute-done.6 = bf16[256,768]{1,0:T(8,128)(2,1)S(1)} collective-permute-done((bf16[256,768]{1,0:T(8,128)(2,1)S(1)}, bf16[256,768]{1,0:T(8,128)(2,1)S(1)}, u32[]{:S(2)}, u32[]{:S(2)}) %collective-permute-start.6) | collective-permute-done | bytes 393248 | tf_op jit(solution)/shard_map/ppermute | solution.py:235
  368.8 5.8 %collective-permute-done.7 = bf16[128,768]{1,0:T(8,128)(2,1)S(1)} collective-permute-done((bf16[128,768]{1,0:T(8,128)(2,1)S(1)}, bf16[128,768]{1,0:T(8,128)(2,1)S(1)}, u32[]{:S(2)}, u32[]{:S(2)}) %collective-permute-start.7) | collective-permute-done | bytes 196640 | tf_op jit(solution)/shard_map/ppermute | solution.py:235
  386.1 51.5 %reduce-scatter.2.cloned.1.call-done = bf16[216,768]{1,0:T(8,128)(2,1)} async-done(((bf16[6912,768]{1,0:T(8,128)(2,1)}), bf16[216,768]{1,0:T(8,128)(2,1)}) %reduce-scatter.2.cloned.1.call-update) | async-done | bytes 331792 | tf_op jit(solution)/shard_map/reduce_scatter | solution.py:325
  446.1 4.8 fusion.79
  453.5 7.3 %fusion.32 = f32[1024,768]{0,1:T(8,128)} fusion(bf16[768,1024]{1,0:T(8,128)(2,1)} %param.22, f32[1024,1024]{1,0:T(8,128)} %get-tuple-element.106, f32[1024,1024]{1,0:T(8,128)} %copy-done.1, f32[1024]{0:T(1024)S(1)} %copy-done.20, f32[1024]{0:T(1024)S(1)} %copy-done.22), kind=kOutput, calls=%fused_computation.76 | convolution fusion | flops 1614807040 | bytes 13115392 | tf_op jit(solution)/shard_map/dot_general | solution.py:46
  478.0 4.9 add_convert_fusion.1
  486.8 12.0 %all-to-all-done.3 = bf16[32,40,288]{2,1,0:T(8,128)(2,1)} async-done(((bf16[32,40,288]{2,1,0:T(8,128)(2,1)}), bf16[32,40,288]{2,1,0:T(8,128)(2,1)}, u32[]{:S(2)}, u32[]{:S(2)}) %all-to-all-start.3) | async-done | bytes 737312 | tf_op jit(solution)/shard_map/all_to_all | solution.py:276
  503.0 5.8 %fusion.74 = (bf16[480,768]{1,0:T(8,128)(2,1)}, f32[480,768]{1,0:T(8,128)}, f32[480,768]{1,0:T(8,128)}, f32[480,768]{1,0:T(8,128)}) fusion(f32[480,768]{1,0:T(8,128)} %param.25, f32[480,768]{1,0:T(8,128)} %reshape.152, f32[480,768]{1,0:T(8,128)} %param.26, f32[480,768]{1,0:T(8,128)} %param.27), kind=kLoop, calls=%fused_computation.175 | loop fusion | flops 5529600 | bytes 11059200 | tf_op jit(solution)/shard_map/convert_element_type | solution.py:484
  (203 shorter events, 119.1 us)
Async XLA Ops:
  7.2 81.2 %copy-start = (bf16[1024,768]{1,0:T(8,128)(2,1)S(1)}, bf16[1024,768]{1,0:T(8,128)(2,1)}, u32[]{:S(2)}) copy-start(bf16[1024,768]{1,0:T(8,128)(2,1)} %param.23) | copy-start | bytes 4718596
  8.8 10.2 %copy-start.23 = (s32[640]{0:T(1024)S(1)}, s32[640]{0:T(1024)}, u32[]{:S(2)}) copy-start(s32[640]{0:T(1024)} %param.24) | copy-start | bytes 7684
  11.6 32.1 %all-to-all-start = ((bf16[32,40,288]{2,1,0:T(8,128)(2,1)}), bf16[32,40,288]{2,1,0:T(8,128)(2,1)S(1)}, u32[]{:S(2)}, u32[]{:S(2)}) async-start(bf16[32,40,288]{2,1,0:T(8,128)(2,1)} %bitcast.50), calls=%async_computation | async-start | bytes 1966080 | tf_op jit(solution)/shard_map/all_to_all | solution.py:276
  18.9 138.9 %all-gather.2.cloned.1.call-start = ((), (), s32[]{:S(2)}) async-start(), calls=%async_computation.5 | async-start | bytes 12165120 | tf_op jit(solution)/shard_map/all_gather | solution.py:307
  44.8 22.3 %copy-start.24 = (f32[352]{0:T(512)S(1)}, f32[352]{0:T(512)}, u32[]{:S(2)}) copy-start(f32[352]{0:T(512)} %param.28) | copy-start | bytes 4228
  67.0 370.6 %reduce-scatter.2.cloned.1.call-start = ((), (), s32[]{:S(2)}) async-start(), calls=%async_computation.6 | async-start | bytes 10948608 | tf_op jit(solution)/shard_map/reduce_scatter | solution.py:325
  67.1 1.2 collective-permute-start
  68.4 3.6 collective-permute-start.1
  72.0 3.7 collective-permute-start.2
  75.7 6.4 %copy-start.31 = (s32[4]{0:T(128)S(1)}, s32[4]{0:T(128)}, u32[]{:S(2)}) copy-start(s32[4]{0:T(128)} %param.19) | copy-start | bytes 52
  75.7 7.0 %copy-start.28 = (s32[4,2]{0,1:T(2,128)S(1)}, s32[4,2]{0,1:T(2,128)}, u32[]{:S(2)}) copy-start(s32[4,2]{0,1:T(2,128)} %param.18) | copy-start | bytes 100
  75.7 8.9 %copy-start.12 = (bf16[1024,768]{1,0:T(8,128)(2,1)S(1)}, bf16[1024,768]{1,0:T(8,128)(2,1)}, u32[]{:S(2)}) copy-start(bf16[1024,768]{1,0:T(8,128)(2,1)} %param.16) | copy-start | bytes 4718596
  75.7 7.2 %collective-permute-start.3 = (bf16[8,352]{1,0:T(8,128)(2,1)S(1)}, bf16[8,352]{1,0:T(8,128)(2,1)S(1)}, u32[]{:S(2)}, u32[]{:S(2)}) collective-permute-start(bf16[8,352]{1,0:T(8,128)(2,1)S(1)} %maximum_select_fusion.2), channel_id=1, source_target_pairs={{0,8},{1,9},{2,10},{3,11},{4,12},{5,13},{6,14},{7,15},{8,0},{9,1},... | collective-permute-start | bytes 16904 | tf_op jit(solution)/shard_map/ppermute | solution.py:235
  82.9 5.2 %collective-permute-start.4 = (bf16[16,352]{1,0:T(8,128)(2,1)S(1)}, bf16[16,352]{1,0:T(8,128)(2,1)S(1)}, u32[]{:S(2)}, u32[]{:S(2)}) collective-permute-start(bf16[16,352]{1,0:T(8,128)(2,1)S(1)} %maximum_select_fusion.1), channel_id=1, source_target_pairs={{0,16},{1,17},{2,18},{3,19},{4,20},{5,21},{6,22},{7,23},{8,24},{9,... | collective-permute-start | bytes 33800 | tf_op jit(solution)/shard_map/ppermute | solution.py:235
  218.4 9.4 %copy-start.32 = (bf16[1024,3072]{1,0:T(8,128)(2,1)}, bf16[1024,3072]{1,0:T(8,128)(2,1)S(1)}, u32[]{:S(2)}) copy-start(bf16[1024,3072]{1,0:T(8,128)(2,1)S(1)} %get-tuple-element.18) | copy-start | bytes 18874372
  229.6 8.4 %slice-start.2 = ((s8[6291456]{0:T(1024)(128)(4,1)}), s8[4194304]{0:T(1024)(128)(4,1)S(1)}, s32[]{:S(2)}) async-start(s8[6291456]{0:T(1024)(128)(4,1)} %bitcast.61), calls=%async_computation.9 | async-start | bytes 8388608
  232.5 5.5 %slice-start.3 = ((s8[6291456]{0:T(1024)(128)(4,1)}), s8[2097152]{0:T(1024)(128)(4,1)S(1)}, s32[]{:S(2)}) async-start(s8[6291456]{0:T(1024)(128)(4,1)} %bitcast.61), calls=%async_computation.10 | async-start | bytes 4194304
  351.0 2.4 collective-permute-start.5
  353.6 13.5 %collective-permute-start.6 = (bf16[256,768]{1,0:T(8,128)(2,1)S(1)}, bf16[256,768]{1,0:T(8,128)(2,1)S(1)}, u32[]{:S(2)}, u32[]{:S(2)}) collective-permute-start(bf16[256,768]{1,0:T(8,128)(2,1)S(1)} %broadcast_select_fusion.2), channel_id=1, source_target_pairs={{0,2},{1,3},{2,0},{3,1},{4,6},{5,7},{6,4},{7,5},{8,10},{9,11},{10,... | collective-permute-start | bytes 1179656 | tf_op jit(solution)/shard_map/ppermute | solution.py:235
  367.3 7.4 %collective-permute-start.7 = (bf16[128,768]{1,0:T(8,128)(2,1)S(1)}, bf16[128,768]{1,0:T(8,128)(2,1)S(1)}, u32[]{:S(2)}, u32[]{:S(2)}) collective-permute-start(bf16[128,768]{1,0:T(8,128)(2,1)S(1)} %broadcast_select_fusion.3), channel_id=1, source_target_pairs={{0,4},{1,5},{2,6},{3,7},{4,0},{5,1},{6,2},{7,3},{8,12},{9,13},{10,... | collective-permute-start | bytes 589832 | tf_op jit(solution)/shard_map/ppermute | solution.py:235
  375.4 4.9 collective-permute-start.8
  380.4 5.1 collective-permute-start.9
  442.2 20.7 %all-to-all-start.2 = ((bf16[32,20,288]{2,1,0:T(8,128)(2,1)}), bf16[32,20,288]{2,1,0:T(8,128)(2,1)}, u32[]{:S(2)}, u32[]{:S(2)}) async-start(bf16[32,20,288]{2,1,0:T(8,128)(2,1)} %bitcast.55), calls=%async_computation.3 | async-start | bytes 1179648 | tf_op jit(solution)/shard_map/all_to_all | solution.py:276
  470.0 28.9 %all-to-all-start.3 = ((bf16[32,40,288]{2,1,0:T(8,128)(2,1)}), bf16[32,40,288]{2,1,0:T(8,128)(2,1)}, u32[]{:S(2)}, u32[]{:S(2)}) async-start(bf16[32,40,288]{2,1,0:T(8,128)(2,1)} %bitcast.54), calls=%async_computation.4 | async-start | bytes 1966080 | tf_op jit(solution)/shard_map/all_to_all | solution.py:276
  (30 other events, 94.3 us)
Sparse Core Ops, SparseCore 0:
  67.2 90.6 all-gather.1
  296.0 141.5 reduce-scatter.1

commit v2 on v1

--- a/solution.py
+++ b/solution.py
@@ -100,22 +100,30 @@
     keys = keys_ref[...].astype(jnp.float32)
     values_t = values_ref[...].astype(jnp.float32).T
     feature = lax.broadcasted_iota(jnp.int32, values_t.shape, 0)
+    operands = []
     for half in range(2):
         _, query_h, keys_h = score_operands(query, keys, bias, lanes, half)
         own = (feature < HEAD_DIM) == (half == 0)
-        values_h = jnp.where(own, values_t, 1.0).astype(jnp.bfloat16)
+        operands.append((query_h, keys_h, jnp.where(own, values_t, 1.0).astype(jnp.bfloat16)))
+    steps = [(half, start) for half in range(2) for start in range(0, rows, TILE)]
+
+    def scores_of(step):
+        half, start = step
+        return product_t(operands[half][1], operands[half][0][start : start + TILE])
+
+    ready = [scores_of(step) for step in steps[:2]]
+    for index, (half, start) in enumerate(steps):
+        if index + 2 < len(steps):
+            ready.append(scores_of(steps[index + 2]))
+        scores = ready.pop(0)
         low = half * HEAD_DIM
         other = HEAD_DIM - low
-        for start in range(0, rows, TILE):
-            scores = product_t(keys_h, query_h[start : start + TILE])
-            highest = jnp.max(scores, axis=0, keepdims=True)
-            raised = jnp.exp(scores - highest).astype(jnp.bfloat16)
-            mixed = product(values_h, raised)
-            summed = mixed[other : other + 1]
-            total_ref[0, half : half + 1, start : start + TILE] = highest + jnp.log(summed)
-            turned[low : low + HEAD_DIM, start : start + TILE] = (
-                mixed[low : low + HEAD_DIM] / summed
-            )
+        highest = jnp.max(scores, axis=0, keepdims=True)
+        raised = jnp.exp(scores - highest).astype(jnp.bfloat16)
+        mixed = product(operands[half][2], raised)
+        summed = mixed[other : other + 1]
+        total_ref[0, half : half + 1, start : start + TILE] = highest + jnp.log(summed)
+        turned[low : low + HEAD_DIM, start : start + TILE] = mixed[low : low + HEAD_DIM] / summed
     context_ref[...] = turned[...].T.astype(jnp.bfloat16)
 
 
@@ -239,18 +247,16 @@
     return (lax.axis_index(AXES) & bit) != 0
 
 
-def gather_small(values, devices):
-    rows = values[None, :]
-    bit = 1
-    while bit < devices:
+def gather_doubling(rows, devices):
+    bit = devices // 2
+    while bit:
         other = exchange(rows, bit, devices)
-        rows = jnp.where(
-            my_bit(bit),
-            jnp.concatenate([other, rows], axis=0),
-            jnp.concatenate([rows, other], axis=0),
+        upper = my_bit(bit)
+        rows = jnp.concatenate(
+            [jnp.where(upper, other, rows), jnp.where(upper, rows, other)], axis=0
         )
-        bit = bit * 2
-    return rows.reshape(-1)
+        bit = bit // 2
+    return rows
 
 
 def reduce_halves(values, devices):
@@ -284,11 +290,18 @@
     return pieces.transpose(1, 0, 2).reshape(-1, D)
 
 
-def route_in(rows, place, slots, devices):
-    pieces = all_to_all(pieces_of(rows, devices)).reshape(slots, -1)
+def route_in(rows, small, place, slots, devices):
+    pieces = pieces_of(rows, devices)
+    piece = pieces.shape[2]
+    extra = -(-small.shape[0] // piece)
+    tail = jnp.pad(small, (0, extra * piece - small.shape[0])).reshape(1, extra, piece)
+    tail = jnp.broadcast_to(tail, (devices, extra, piece))
+    moved = all_to_all(jnp.concatenate([pieces, tail], axis=1))
+    small_all = moved[:, -extra:].reshape(devices, -1)[:, : small.shape[0]].reshape(-1)
+    pieces = moved[:, :-extra].reshape(slots, piece)
     chosen = place[:, None] == jnp.arange(slots, dtype=jnp.int32)[None, :]
     homed = product(chosen.astype(jnp.bfloat16), pieces).astype(jnp.bfloat16)
-    return rows_of(all_to_all(homed.reshape(devices, -1, pieces.shape[1])))
+    return (rows_of(all_to_all(homed.reshape(devices, -1, piece))), small_all)
 
 
 def route_out(rows, place, slots, devices):
@@ -298,49 +311,101 @@
     return rows_of(all_to_all(slotted.reshape(devices, -1, pieces.shape[1])))
 
 
-def gather_rows(weights, slot, devices):
-    blocks = slot.shape[0]
+KEY_BLOCKS = D // BLOCK_ROWS
+
+
+def even_homes(blocks, devices):
+    return KEY_BLOCKS % devices == 0 and (blocks - 2 * KEY_BLOCKS) % devices == 0
+
+
+def home_order(slot, devices, turned_groups):
+    order = jnp.array(reverse_bits(devices), dtype=jnp.int32)
+    parts = []
+    for group in range(turned_groups):
+        part = slot[group * KEY_BLOCKS : (group + 1) * KEY_BLOCKS]
+        parts.append(part.reshape(devices, -1)[order])
+    parts.append(slot[turned_groups * KEY_BLOCKS :].reshape(devices, -1))
+    return jnp.concatenate(parts, axis=1).reshape(-1)
+
+
+def gather_rows(weights, small, slot, devices):
     slots = devices * (weights.shape[0] // BLOCK_ROWS)
     low = weights.astype(jnp.bfloat16)
-    if blocks % devices == 0 and (BLOCK_ROWS * D) % devices == 0:
-        homed = route_in(low, slot, slots, devices)
-        rows = lax.all_gather(homed, AXES, axis=0, tiled=True)
-        return (rows[:D], rows[D : 2 * D], rows[2 * D : 2 * D + FF], rows[2 * D + FF :])
-    return unpack_rows(lax.all_gather(low, AXES, axis=0, tiled=True), slot)
-
-
-def scatter_grads(grad_key, grad_rest, small_grad, slot, slots, devices):
-    key_blocks = D // BLOCK_ROWS
+    small = small.astype(jnp.bfloat16)
+    if not even_homes(slot.shape[0], devices):
+        rows = unpack_rows(lax.all_gather(low, AXES, axis=0, tiled=True), slot)
+        return (rows, lax.all_gather(small, AXES, axis=0, tiled=True))
+    homed, small_all = route_in(low, small, home_order(slot, devices, 1), slots, devices)
+    share = D // devices
+    rest = lax.all_gather(homed[share:], AXES, axis=0, tiled=True)
+    keys = gather_doubling(homed[:share], devices)
+    return ((keys, rest[:D], rest[D : D + FF], rest[D + FF :]), small_all)
+
+
+def weight_grads_kernel(pre_ref, hidden_ref, active_ref, branch_ref, out_ref):
+    step = pl.program_id(0)
+    half = pl.num_programs(0) // 2
+
+    @pl.when(step < half)
+    def _():
+        out_ref[...] = inner_rows(pre_ref[...], hidden_ref[...]).astype(jnp.bfloat16)
+
+    @pl.when(step >= half)
+    def _():
+        out_ref[...] = inner_rows(active_ref[...], branch_ref[...]).astype(jnp.bfloat16)
+
+
+def weight_grads(grad_pre, hidden_low, active, grad_branch):
+    rows = grad_pre.shape[0]
+    width = 512
+    half = FF // width
+    whole = pl.BlockSpec((rows, D), lambda i: (0, 0))
+    return pl.pallas_call(
+        weight_grads_kernel,
+        out_shape=jax.ShapeDtypeStruct((2 * FF, D), jnp.bfloat16),
+        grid=(2 * half,),
+        in_specs=[
+            pl.BlockSpec((rows, width), lambda i: (0, jnp.minimum(i, half - 1))),
+            whole,
+            pl.BlockSpec((rows, width), lambda i: (0, jnp.maximum(i - half, 0))),
+            whole,
+        ],
+        out_specs=pl.BlockSpec((width, D), lambda i: (i, 0)),
+        name="weight_grads",
+    )(grad_pre, hidden_low, active, grad_branch)
+
+
+def scatter_grads(grad_key, grad_out, grad_wide, small_grad, slot, slots, devices):
     blocks = slot.shape[0]
-    share = small_grad.shape[0] // devices
-    if key_blocks % devices or (blocks - key_blocks) % devices or share > D:
-        rows = jnp.concatenate([grad_key, *grad_rest], axis=0).reshape(blocks, BLOCK_ROWS * D)
+    if not even_homes(blocks, devices):
+        rows = jnp.concatenate([grad_key, grad_out, grad_wide], axis=0)
+        rows = rows.reshape(blocks, BLOCK_ROWS * D)
         chosen = slot[:, None] == jnp.arange(slots, dtype=jnp.int32)[None, :]
         slotted = inner_rows(chosen.astype(jnp.bfloat16), rows).astype(jnp.bfloat16)
         return (
             lax.psum_scatter(slotted.reshape(-1, D), AXES, scatter_dimension=0, tiled=True),
             lax.psum_scatter(small_grad, AXES, scatter_dimension=0, tiled=True),
         )
-    rest = jnp.concatenate(grad_rest, axis=0)
-    rest_home = lax.psum_scatter(rest, AXES, scatter_dimension=0, tiled=True)
+    wide_home = lax.psum_scatter(grad_wide, AXES, scatter_dimension=0, tiled=True)
     order = jnp.array(reverse_bits(devices), dtype=jnp.int32)
-    key_rows = D // devices
-    wide = -(-(key_rows + 1) // 16) * 16
-    small_rows = small_grad.reshape(devices, share)[order].astype(jnp.bfloat16)
-    small_rows = jnp.pad(small_rows[:, None, :], ((0, 0), (0, wide - key_rows - 1), (0, D - share)))
-    packed = jnp.concatenate([grad_key.reshape(devices, key_rows, D), small_rows], axis=1)
+    share = D // devices
+    small_share = small_grad.shape[0] // devices
+    small_deep = -(-small_share // D)
+    deep = -(-(2 * share + small_deep) // 8) * 8
+    small_rows = small_grad.reshape(devices, small_share)[order].astype(jnp.bfloat16)
+    small_rows = jnp.pad(
+        small_rows, ((0, 0), (0, (deep - 2 * share) * D - small_share))
+    ).reshape(devices, -1, D)
+    packed = jnp.concatenate(
+        [grad_key.reshape(devices, share, D), grad_out.reshape(devices, share, D), small_rows],
+        axis=1,
+    )
     summed = reduce_halves(packed.reshape(-1, D), devices)
-    home = jnp.concatenate([summed[:key_rows], rest_home], axis=0)
-    place = jnp.concatenate(
-        [
-            slot[:key_blocks].reshape(devices, -1)[order],
-            slot[key_blocks:].reshape(devices, -1),
-        ],
-        axis=1,
-    ).reshape(-1)
+    home = jnp.concatenate([summed[: 2 * share], wide_home], axis=0)
+    small_home = summed[2 * share : 2 * share + small_deep].reshape(-1)[:small_share]
     return (
-        route_out(home, place, slots, devices).astype(jnp.float32),
-        summed[key_rows, :share].astype(jnp.float32),
+        route_out(home, home_order(slot, devices, 2), slots, devices).astype(jnp.float32),
+        small_home.astype(jnp.float32),
     )
 
 
@@ -372,8 +437,9 @@
     capacity = weights.shape[0] // BLOCK_ROWS
     devices = lax.axis_size("rows") * lax.axis_size("heads")
     slot = slot_index(owner, capacity)
-    small_all = gather_small(small_weights.astype(jnp.bfloat16), devices)
-    key_rows, out_rows, up_rows, down_rows = gather_rows(weights, slot, devices)
+    (key_rows, out_rows, up_rows, down_rows), small_all = gather_rows(
+        weights, small_weights, slot, devices
+    )
     (
         scale_q_rank,
         scale_v_rank,
@@ -419,10 +485,9 @@
     grad_second = norm_back(grad_top * gain_two, norm_two, inverse_two)
     grad_branch = grad_second.astype(jnp.bfloat16)
     grad_down_bias = jnp.sum(grad_branch.astype(jnp.float32), axis=0)
-    grad_down = inner_rows(active, grad_branch).astype(jnp.bfloat16)
     grad_pre = (product_t(grad_branch, down_rows) * slope.astype(jnp.float32)).astype(jnp.bfloat16)
     grad_up_bias = jnp.sum(grad_pre.astype(jnp.float32), axis=0)
-    grad_up = inner_rows(grad_pre, hidden_low).astype(jnp.bfloat16)
+    grad_wide = weight_grads(grad_pre, hidden_low, active, grad_branch)
     grad_hidden = grad_second + product(grad_pre, up_rows)
     grad_gain_one = jnp.sum(grad_hidden * norm_one, axis=0)
     grad_shift_one = jnp.sum(grad_hidden, axis=0)
@@ -467,7 +532,7 @@
         ]
     )
     owned_grad, owned_small = scatter_grads(
-        grad_key, (grad_out, grad_up, grad_down), small_grad, slot, devices * capacity, devices
+        grad_key, grad_out, grad_wide, small_grad, slot, devices * capacity, devices
     )
     new_weights, new_first, new_second = adamw_update(
         weights, first_moment, second_moment, owned_grad, 0.01, 0.03

time: 522 us -> 453 us (0.87)
  matrix products: 126 us -> 95.6 us
  other arithmetic: 45.6 us -> 23.8 us
  waiting for transfers between devices: 175 us -> 159 us
    ppermute x10, waiting for transfers between devices: 28.1 us -> 69.7 us  [exchange(): return lax.ppermute(values, AXES, [(i, i ^ bit) for i in range(devices)])]
    all_gather x1, waiting for transfers between devices: 57.4 us -> 22 us  [gather_rows(): rest = lax.all_gather(homed[share:], AXES, axis=0, tiled=True)]
    reduce_scatter x1, waiting for transfers between devices: 51.5 us -> 18.5 us  [scatter_grads(): lax.psum_scatter(grad_wide, AXES, scatter_dimension=0, tiled=True)]
    concatenate x4 -> x8, other arithmetic: 23.4 us -> 2.5 us  [the longest x1 1.16 us: route_in(): moved = all_to_all(jnp.concatenate([pieces, tail], axis=1))]
    pallas_call x0 -> x1, Pallas kernels: none -> 18.6 us  [weight_grads(): pl.pallas_call(weight_grads_kernel, out_shape=jax.ShapeDtypeStruct((2 * F...]
    pallas_call x1, Pallas kernels: 37.9 us -> 22.2 us  [attend_forward(): pl.pallas_call(attend_forward_kernel, out_shape=(jax.ShapeDtypeStruct((ro...]
    dot_general x5 -> x3, matrix products: 23.5 us -> 7.87 us  [inner_rows(): lax.dot_general(left, right, (((0,), (0,)), ((), ())), preferred_element_...]
    all_to_all x3, waiting for transfers between devices: 38.5 us -> 49.2 us  [all_to_all(): return lax.all_to_all(values, AXES, split_axis=0, concat_axis=0, tiled=True)]
  transfers between devices with their start and end apart: 15 -> 15, of which waited for: 13 -> 14; matrix products, arithmetic and copies ran while one was open for 14% -> 17% of each run, Pallas kernels for 7% -> 13%
where the time goes in v2:
time: 453 us; the launch traced here: 447 us
  waiting for transfers between devices  159 us (35%)
  matrix products  95.6 us (21%)
  Pallas kernels  75.1 us (17%)
  local copies, waits for them, and re-layouts  31.8 us (7%)
  starting transfers between devices  25.6 us (6%)
  other arithmetic  23.8 us (5%)
  blocking collectives  20.4 us (5%)
  between operations  15.4 us (3%)
    ppermute x10, waiting for transfers between devices, exchange(): return lax.ppermute(values, AXES, [(i, i ^ bit) for i in range(devices)])  69.7 us
    all_to_all x3, waiting for transfers between devices, all_to_all(): return lax.all_to_all(values, AXES, split_axis=0, concat_axis=0, tiled=True)  49.2 us
    dot_general x9, matrix products, product_t(): lax.dot_general(left, right, (((1,), (1,)), ((), ())), preferred_element_...  46.9 us
    dot_general x10, matrix products, product(): return jnp.dot(left, right, preferred_element_type=jnp.float32)  40.8 us
    pallas_call x1, Pallas kernels, attend_backward(): pl.pallas_call(attend_backward_kernel, out_shape=(shape, shape, shape), g...  34.4 us
    pallas_call x1, Pallas kernels, attend_forward(): pl.pallas_call(attend_forward_kernel, out_shape=(jax.ShapeDtypeStruct((ro...  22.2 us
    all_gather x1, waiting for transfers between devices, gather_rows(): rest = lax.all_gather(homed[share:], AXES, axis=0, tiled=True)  22 us
    all_to_all x1, blocking collectives, all_to_all(): return lax.all_to_all(values, AXES, split_axis=0, concat_axis=0, tiled=True)  20.4 us
  transfers between devices with their start and end apart: 15, of which 14 were waited for; matrix products, arithmetic and copies ran while one was open for 17% of the time, Pallas kernels for 13%

profile of v2, /device:TPU:0, one launch (start us, length us, event | category | flops | bytes accessed | tf_op | source)
XLA Modules:
  0.0 447.2 jit_solution(14136360837319666489)
XLA Ops:
  12.0 7.3 %all-to-all-start = ((bf16[32,42,288]{2,1,0:T(8,128)(2,1)}), bf16[32,42,288]{2,1,0:T(8,128)(2,1)S(1)}, u32[]{:S(2)}, u32[]{:S(2)}) async-start(bf16[32,42,288]{2,1,0:T(8,128)(2,1)} %pad_maximum_fusion.1), calls=%async_computation | async-start | bytes 2359296 | tf_op jit(solution)/shard_map/all_to_all | solution.py:282
  21.6 26.7 %all-to-all-done = bf16[32,42,288]{2,1,0:T(8,128)(2,1)S(1)} async-done(((bf16[32,42,288]{2,1,0:T(8,128)(2,1)}), bf16[32,42,288]{2,1,0:T(8,128)(2,1)S(1)}, u32[]{:S(2)}, u32[]{:S(2)}) %all-to-all-start) | async-done | bytes 774176 | tf_op jit(solution)/shard_map/all_to_all | solution.py:282
  52.5 20.4 %all_to_all.20 = bf16[32,20,288]{2,1,0:T(8,128)(2,1)S(1)} all-to-all(bf16[32,20,288]{2,1,0:T(8,128)(2,1)} %reshape.168), channel_id=1, replica_groups=mesh['rows'=8,'heads'=4] {'rows','heads'}, dimensions={0} | all-to-all | bytes 737280 | tf_op jit(solution)/shard_map/all_to_all | solution.py:282
  78.7 5.1 %convolution_convert_fusion = bf16[1024,1024]{1,0:T(8,128)(2,1)} fusion(bf16[1024,768]{1,0:T(8,128)(2,1)} %param.18, bf16[768,1024]{1,0:T(8,128)(2,1)} %param.24), kind=kOutput, calls=%fused_computation.83 | convolution fusion | flops 1611661312 | bytes 5242880 | tf_op jit(solution)/shard_map/dot_general | solution.py:42
  91.8 5.0 %collective-permute-done.1 = bf16[48,768]{1,0:T(8,128)(2,1)S(1)} collective-permute-done((bf16[48,768]{1,0:T(8,128)(2,1)S(1)}, bf16[48,768]{1,0:T(8,128)(2,1)S(1)}, u32[]{:S(2)}, u32[]{:S(2)}) %collective-permute-start.1) | collective-permute-done | bytes 73760 | tf_op jit(solution)/shard_map/ppermute | solution.py:243
  105.5 9.2 %collective-permute-done.3 = bf16[192,768]{1,0:T(8,128)(2,1)S(1)} collective-permute-done((bf16[192,768]{1,0:T(8,128)(2,1)S(1)}, bf16[192,768]{1,0:T(8,128)(2,1)S(1)}, u32[]{:S(2)}, u32[]{:S(2)}) %collective-permute-start.3) | collective-permute-done | bytes 294944 | tf_op jit(solution)/shard_map/ppermute | solution.py:243
  121.4 22.2 %attend_forward.1 = (bf16[1024,768]{1,0:T(8,128)(2,1)}, f32[6,2,1024]{2,1,0:T(2,128)}) custom-call(s32[3]{0:T(128)} %pad_add_fusion.2.spans, bf16[1024,768]{1,0:T(8,128)(2,1)} %add_convert_fusion.4.query_ref, bf16[1024,768]{1,0:T(8,128)(2,1)} %fusion.55.keys_ref, bf16[1024,768]{1,0:T(8,128)(2,1)} %add_convert_fusion.3.values_ref), custom_call_target="tpu_custom_call" | custom-call | tf_op jit(solution)/shard_map/attend_forward/pallas_call | solution.py:199
  143.6 22.0 %all-gather.2.cloned.1.call-done = bf16[6912,768]{1,0:T(8,128)(2,1)} async-done(((bf16[216,768]{1,0:T(8,128)(2,1)}), bf16[6912,768]{1,0:T(8,128)(2,1)}) %all-gather.2.cloned.1.call-update) | async-done | bytes 10616848 | tf_op jit(solution)/shard_map/all_gather | solution.py:340
  171.8 11.8 %fusion.4 = (bf16[1024,3072]{1,0:T(8,128)(2,1)S(1)}, bf16[1024,3072]{1,0:T(8,128)(2,1)S(1)}) fusion(f32[3072]{0:T(1024)S(1)} %slice_convert_fusion, bf16[1024,768]{1,0:T(8,128)(2,1)S(1)} %fusion.29.hidden_ref, bf16[6912,768]{1,0:T(8,128)(2,1)S(1)} %copy-done.37), kind=kOutput, calls=%fused_computation.8 | convolution fusion | flops 4869586944 | bytes 18886656 | tf_op jit(solution)/shard_map/dot_general | solution.py:46
  183.7 5.4 %fusion.74 = (f32[1024]{0:T(1024)S(1)}, f32[1024,768]{1,0:T(8,128)S(1)}) fusion(f32[768]{0:T(1024)S(1)} %get-tuple-element.63, bf16[1024,3072]{1,0:T(8,128)(2,1)S(1)} %get-tuple-element.18.active_ref, bf16[6912,768]{1,0:T(8,128)(2,1)S(1)} %copy-done.37, f32[768]{0:T(1024)S(1)} %get-tuple-element.64, f32[768]{0:T(1024)S(1)} %get-tuple-element.65, ...), kind=kOutput, calls=%fused_computation.184 | convolution fusion | flops 4837342208 | bytes 17326080 | tf_op jit(solution)/shard_map/dot_general | solution.py:42
  196.0 7.1 %convert_reduce_fusion = (f32[3072]{0:T(1024)S(1)}, bf16[1024,3072]{1,0:T(8,128)(2,1)}) fusion(bf16[1024,3072]{1,0:T(8,128)(2,1)S(1)} %get-tuple-element.19, bf16[1024,768]{1,0:T(8,128)(2,1)S(1)} %get-tuple-element.43.branch_ref, bf16[6912,768]{1,0:T(8,128)(2,1)S(1)} %copy-done.37), kind=kOutput, calls=%fused_computation.9 | convolution fusion | flops 4847563776 | bytes 18886656 | tf_op jit(solution)/shard_map/dot_general | solution.py:46
  203.1 18.6 %weight_grads.1 = bf16[6144,768]{1,0:T(8,128)(2,1)} custom-call(bf16[1024,3072]{1,0:T(8,128)(2,1)} %get-tuple-element.82.pre_ref, bf16[1024,768]{1,0:T(8,128)(2,1)} %copy-done.11, bf16[1024,3072]{1,0:T(8,128)(2,1)} %copy-done.13, bf16[1024,768]{1,0:T(8,128)(2,1)} %copy-done.12), custom_call_target="tpu_custom_call" | custom-call | tf_op jit(solution)/shard_map/weight_grads/pallas_call | solution.py:363
  221.7 11.5 %multiply_reduce_fusion = (f32[768]{0:T(1024)S(1)}, f32[1024]{0:T(1024)S(1)}, f32[1024]{0:T(1024)S(1)}, f32[768]{0:T(1024)S(1)}, f32[1024,768]{1,0:T(8,128)S(1)}) fusion(f32[1024,768]{1,0:T(8,128)} %copy-done.1, f32[1024]{0:T(1024)S(1)} %add_rsqrt_fusion.1, f32[1024]{0:T(1024)S(1)} %broadcast_multiply_fusion.5, f32[768]{0:T(1024)S(1)} %get-tuple-element.65, ...), kind=kOutput, calls=%fused_computation.51 | convolution fusion | flops 4845989888 | bytes 22065152 | tf_op jit(solution)/shard_map/dot_general | solution.py:42
  234.3 4.9 %convolution_convert_fusion.2.grad_ref = bf16[1024,768]{1,0:T(8,128)(2,1)} fusion(bf16[6912,768]{1,0:T(8,128)(2,1)} %all-gather.2.cloned.1.call-done, f32[1024,768]{1,0:T(8,128)S(1)} %get-tuple-element.45), kind=kOutput, calls=%fused_computation.86 | convolution fusion | flops 1209532416 | bytes 5898240 | tf_op jit(solution)/shard_map/dot_general | solution.py:46
  239.2 34.4 %attend_backward.1 = (bf16[1024,768]{1,0:T(8,128)(2,1)}, bf16[1024,768]{1,0:T(8,128)(2,1)}, bf16[1024,768]{1,0:T(8,128)(2,1)}) custom-call(s32[3]{0:T(128)} %pad_add_fusion.2.spans, bf16[1024,768]{1,0:T(8,128)(2,1)} %add_convert_fusion.4.query_ref, bf16[1024,768]{1,0:T(8,128)(2,1)} %fusion.55.keys_ref, bf16[1024,768]{1,0:T(8,128)(2,1)} %add_convert_fusion.3.values_ref, ...), custom_call_target="tpu_custom_call" | custom-call | tf_op jit(solution)/shard_map/attend_backward/pallas_call | solution.py:221
  295.6 24.0 %collective-permute-done.6 = bf16[448,768]{1,0:T(8,128)(2,1)S(1)} collective-permute-done((bf16[448,768]{1,0:T(8,128)(2,1)S(1)}, bf16[448,768]{1,0:T(8,128)(2,1)S(1)}, u32[]{:S(2)}, u32[]{:S(2)}) %collective-permute-start.6) | collective-permute-done | bytes 688160 | tf_op jit(solution)/shard_map/ppermute | solution.py:243
  321.4 11.5 %collective-permute-done.7 = bf16[224,768]{1,0:T(8,128)(2,1)S(1)} collective-permute-done((bf16[224,768]{1,0:T(8,128)(2,1)S(1)}, bf16[224,768]{1,0:T(8,128)(2,1)S(1)}, u32[]{:S(2)}, u32[]{:S(2)}) %collective-permute-start.7) | collective-permute-done | bytes 344096 | tf_op jit(solution)/shard_map/ppermute | solution.py:243
  334.3 7.8 %collective-permute-done.8 = bf16[112,768]{1,0:T(8,128)(2,1)S(1)} collective-permute-done((bf16[112,768]{1,0:T(8,128)(2,1)S(1)}, bf16[112,768]{1,0:T(8,128)(2,1)S(1)}, u32[]{:S(2)}, u32[]{:S(2)}) %collective-permute-start.8) | collective-permute-done | bytes 172064 | tf_op jit(solution)/shard_map/ppermute | solution.py:243
  344.8 4.8 %collective-permute-done.9 = bf16[56,768]{1,0:T(8,128)(2,1)S(1)} collective-permute-done((bf16[56,768]{1,0:T(8,128)(2,1)S(1)}, bf16[56,768]{1,0:T(8,128)(2,1)S(1)}, u32[]{:S(2)}, u32[]{:S(2)}) %collective-permute-start.9) | collective-permute-done | bytes 86048 | tf_op jit(solution)/shard_map/ppermute | solution.py:243
  350.9 18.5 %reduce-scatter.2.cloned.1.call-done = bf16[192,768]{1,0:T(8,128)(2,1)} async-done(((bf16[6144,768]{1,0:T(8,128)(2,1)}), bf16[192,768]{1,0:T(8,128)(2,1)}) %reduce-scatter.2.cloned.1.call-update) | async-done | bytes 294928 | tf_op jit(solution)/shard_map/reduce_scatter | solution.py:389
  377.9 5.0 %fusion.75 = f32[1024,768]{1,0:T(8,128)} fusion(bf16[1024,768]{1,0:T(8,128)(2,1)} %get-tuple-element.21, bf16[768,768]{1,0:T(8,128)(2,1)} %param.22), kind=kOutput, calls=%fused_computation.185 | convolution fusion | flops 1207959552 | bytes 5898240 | tf_op jit(solution)/shard_map/dot_general | solution.py:46
  387.0 7.6 %all-to-all-done.2 = bf16[32,20,288]{2,1,0:T(8,128)(2,1)} async-done(((bf16[32,20,288]{2,1,0:T(8,128)(2,1)}), bf16[32,20,288]{2,1,0:T(8,128)(2,1)}, u32[]{:S(2)}, u32[]{:S(2)}) %all-to-all-start.2) | async-done | bytes 368672 | tf_op jit(solution)/shard_map/all_to_all | solution.py:282
  415.0 14.9 %all-to-all-done.3 = bf16[32,40,288]{2,1,0:T(8,128)(2,1)} async-done(((bf16[32,40,288]{2,1,0:T(8,128)(2,1)}), bf16[32,40,288]{2,1,0:T(8,128)(2,1)}, u32[]{:S(2)}, u32[]{:S(2)}) %all-to-all-start.3) | async-done | bytes 737312 | tf_op jit(solution)/shard_map/all_to_all | solution.py:282
  434.1 5.8 %fusion.69 = (bf16[480,768]{1,0:T(8,128)(2,1)}, f32[480,768]{1,0:T(8,128)}, f32[480,768]{1,0:T(8,128)}, f32[480,768]{1,0:T(8,128)}) fusion(f32[480,768]{1,0:T(8,128)} %param.27, f32[480,768]{1,0:T(8,128)} %reshape.177, f32[480,768]{1,0:T(8,128)} %param.28, f32[480,768]{1,0:T(8,128)} %param.29), kind=kLoop, calls=%fused_computation.181 | loop fusion | flops 5529600 | bytes 11059200 | tf_op jit(solution)/shard_map/convert_element_type | solution.py:549
  (222 shorter events, 120.3 us)
Async XLA Ops:
  7.2 77.5 %copy-start = (bf16[1024,768]{1,0:T(8,128)(2,1)S(1)}, bf16[1024,768]{1,0:T(8,128)(2,1)}, u32[]{:S(2)}) copy-start(bf16[1024,768]{1,0:T(8,128)(2,1)} %param.25) | copy-start | bytes 4718596
  12.0 36.3 %all-to-all-start = ((bf16[32,42,288]{2,1,0:T(8,128)(2,1)}), bf16[32,42,288]{2,1,0:T(8,128)(2,1)S(1)}, u32[]{:S(2)}, u32[]{:S(2)}) async-start(bf16[32,42,288]{2,1,0:T(8,128)(2,1)} %pad_maximum_fusion.1), calls=%async_computation | async-start | bytes 2359296 | tf_op jit(solution)/shard_map/all_to_all | solution.py:282
  19.3 146.3 %all-gather.2.cloned.1.call-start = ((), (), s32[]{:S(2)}) async-start(), calls=%async_computation.5 | async-start | bytes 10948608 | tf_op jit(solution)/shard_map/all_gather | solution.py:340
  50.2 26.4 %copy-start.35 = (s32[4,2]{0,1:T(2,128)S(1)}, s32[4,2]{0,1:T(2,128)}, u32[]{:S(2)}) copy-start(s32[4,2]{0,1:T(2,128)} %param.20) | copy-start | bytes 100
  50.2 26.6 %copy-start.41 = (s32[4]{0:T(128)S(1)}, s32[4]{0:T(128)}, u32[]{:S(2)}) copy-start(s32[4]{0:T(128)} %param.21) | copy-start | bytes 52
  76.4 293.0 %reduce-scatter.2.cloned.1.call-start = ((), (), s32[]{:S(2)}) async-start(), calls=%async_computation.6 | async-start | bytes 9732096 | tf_op jit(solution)/shard_map/reduce_scatter | solution.py:389
  84.2 7.4 %collective-permute-start = (bf16[24,768]{1,0:T(8,128)(2,1)S(1)}, bf16[24,768]{1,0:T(8,128)(2,1)S(1)}, u32[]{:S(2)}, u32[]{:S(2)}) collective-permute-start(bf16[24,768]{1,0:T(8,128)(2,1)S(1)} %slice.156), channel_id=1, source_target_pairs={{0,16},{1,17},{2,18},{3,19},{4,20},{5,21},{6,22},{7,23},{8,24},{9,... | collective-permute-start | bytes 110600 | tf_op jit(solution)/shard_map/ppermute | solution.py:243
  84.7 13.4 %copy-start.38 = (bf16[1024,768]{1,0:T(8,128)(2,1)S(1)}, bf16[1024,768]{1,0:T(8,128)(2,1)}, u32[]{:S(2)}) copy-start(bf16[1024,768]{1,0:T(8,128)(2,1)} %param.18) | copy-start | bytes 4718596
  84.7 13.4 %copy-start.40 = (bf16[768,768]{1,0:T(8,128)(2,1)S(1)}, bf16[768,768]{1,0:T(8,128)(2,1)}, u32[]{:S(2)}) copy-start(bf16[768,768]{1,0:T(8,128)(2,1)} %param.23) | copy-start | bytes 3538948
  88.3 12.5 %copy-start.17 = (f32[1024,768]{1,0:T(8,128)}, f32[1024,768]{1,0:T(8,128)S(1)}, u32[]{:S(2)}) copy-start(f32[1024,768]{1,0:T(8,128)S(1)} %fusion.33) | copy-start | bytes 9437188
  91.7 5.1 %collective-permute-start.1 = (bf16[48,768]{1,0:T(8,128)(2,1)S(1)}, bf16[48,768]{1,0:T(8,128)(2,1)S(1)}, u32[]{:S(2)}, u32[]{:S(2)}) collective-permute-start(bf16[48,768]{1,0:T(8,128)(2,1)S(1)} %pad_maximum_fusion.9), channel_id=1, source_target_pairs={{0,8},{1,9},{2,10},{3,11},{4,12},{5,13},{6,14},{7,15},{8,0},{9,1},... | collective-permute-start | bytes 221192 | tf_op jit(solution)/shard_map/ppermute | solution.py:243
  96.9 5.2 %collective-permute-start.2 = (bf16[96,768]{1,0:T(8,128)(2,1)S(1)}, bf16[96,768]{1,0:T(8,128)(2,1)S(1)}, u32[]{:S(2)}, u32[]{:S(2)}) collective-permute-start(bf16[96,768]{1,0:T(8,128)(2,1)S(1)} %pad_maximum_fusion.8), channel_id=1, source_target_pairs={{0,4},{1,5},{2,6},{3,7},{4,0},{5,1},{6,2},{7,3},{8,12},{9,13},{10,... | collective-permute-start | bytes 442376 | tf_op jit(solution)/shard_map/ppermute | solution.py:243
  102.1 12.6 %collective-permute-start.3 = (bf16[192,768]{1,0:T(8,128)(2,1)S(1)}, bf16[192,768]{1,0:T(8,128)(2,1)S(1)}, u32[]{:S(2)}, u32[]{:S(2)}) collective-permute-start(bf16[192,768]{1,0:T(8,128)(2,1)S(1)} %pad_maximum_fusion.7), channel_id=1, source_target_pairs={{0,2},{1,3},{2,0},{3,1},{4,6},{5,7},{6,4},{7,5},{8,10},{9,11},{10,... | collective-permute-start | bytes 884744 | tf_op jit(solution)/shard_map/ppermute | solution.py:243
  105.5 12.0 %copy-start.19 = (f32[1024,768]{1,0:T(8,128)}, f32[1024,768]{1,0:T(8,128)S(1)}, u32[]{:S(2)}) copy-start(f32[1024,768]{1,0:T(8,128)S(1)} %fusion.35) | copy-start | bytes 9437188
  114.9 2.7 collective-permute-start.4
  169.5 14.2 %copy-start.1 = (f32[1024,768]{1,0:T(8,128)}, f32[1024,768]{1,0:T(8,128)S(1)}, u32[]{:S(2)}) copy-start(f32[1024,768]{1,0:T(8,128)S(1)} %get-tuple-element.76) | copy-start | bytes 9437188
  171.8 11.9 %copy-start.11 = (bf16[1024,768]{1,0:T(8,128)(2,1)}, bf16[1024,768]{1,0:T(8,128)(2,1)S(1)}, u32[]{:S(2)}) copy-start(bf16[1024,768]{1,0:T(8,128)(2,1)S(1)} %fusion.29.hidden_ref) | copy-start | bytes 4718596
  290.4 3.2 collective-permute-start.5
  294.1 25.4 %collective-permute-start.6 = (bf16[448,768]{1,0:T(8,128)(2,1)S(1)}, bf16[448,768]{1,0:T(8,128)(2,1)S(1)}, u32[]{:S(2)}, u32[]{:S(2)}) collective-permute-start(bf16[448,768]{1,0:T(8,128)(2,1)S(1)} %broadcast_select_fusion.2), channel_id=1, source_target_pairs={{0,2},{1,3},{2,0},{3,1},{4,6},{5,7},{6,4},{7,5},{8,10},{9,11},{10,... | collective-permute-start | bytes 2064392 | tf_op jit(solution)/shard_map/ppermute | solution.py:243
  319.9 13.0 %collective-permute-start.7 = (bf16[224,768]{1,0:T(8,128)(2,1)S(1)}, bf16[224,768]{1,0:T(8,128)(2,1)S(1)}, u32[]{:S(2)}, u32[]{:S(2)}) collective-permute-start(bf16[224,768]{1,0:T(8,128)(2,1)S(1)} %broadcast_select_fusion.5), channel_id=1, source_target_pairs={{0,4},{1,5},{2,6},{3,7},{4,0},{5,1},{6,2},{7,3},{8,12},{9,13},{10,... | collective-permute-start | bytes 1032200 | tf_op jit(solution)/shard_map/ppermute | solution.py:243
  333.1 9.0 %collective-permute-start.8 = (bf16[112,768]{1,0:T(8,128)(2,1)S(1)}, bf16[112,768]{1,0:T(8,128)(2,1)S(1)}, u32[]{:S(2)}, u32[]{:S(2)}) collective-permute-start(bf16[112,768]{1,0:T(8,128)(2,1)S(1)} %broadcast_select_fusion.8), channel_id=1, source_target_pairs={{0,8},{1,9},{2,10},{3,11},{4,12},{5,13},{6,14},{7,15},{8,0},{9,1},... | collective-permute-start | bytes 516104 | tf_op jit(solution)/shard_map/ppermute | solution.py:243
  342.2 7.4 %collective-permute-start.9 = (bf16[56,768]{1,0:T(8,128)(2,1)S(1)}, bf16[56,768]{1,0:T(8,128)(2,1)S(1)}, u32[]{:S(2)}, u32[]{:S(2)}) collective-permute-start(bf16[56,768]{1,0:T(8,128)(2,1)S(1)} %broadcast_select_fusion.11), channel_id=1, source_target_pairs={{0,16},{1,17},{2,18},{3,19},{4,20},{5,21},{6,22},{7,23},{8,24},{9,... | collective-permute-start | bytes 258056 | tf_op jit(solution)/shard_map/ppermute | solution.py:243
  373.9 20.7 %all-to-all-start.2 = ((bf16[32,20,288]{2,1,0:T(8,128)(2,1)}), bf16[32,20,288]{2,1,0:T(8,128)(2,1)}, u32[]{:S(2)}, u32[]{:S(2)}) async-start(bf16[32,20,288]{2,1,0:T(8,128)(2,1)} %bitcast.54), calls=%async_computation.3 | async-start | bytes 1179648 | tf_op jit(solution)/shard_map/all_to_all | solution.py:282
  401.8 28.1 %all-to-all-start.3 = ((bf16[32,40,288]{2,1,0:T(8,128)(2,1)}), bf16[32,40,288]{2,1,0:T(8,128)(2,1)}, u32[]{:S(2)}, u32[]{:S(2)}) async-start(bf16[32,40,288]{2,1,0:T(8,128)(2,1)} %bitcast.50), calls=%async_computation.4 | async-start | bytes 1966080 | tf_op jit(solution)/shard_map/all_to_all | solution.py:282
  (33 other events, 157.9 us)
Sparse Core Ops, SparseCore 0:
  76.5 89.0 all-gather.1
  221.8 147.5 reduce-scatter.1

commit v3 on v2

--- a/solution.py
+++ b/solution.py
@@ -248,34 +248,29 @@
 
 
 def gather_doubling(rows, devices):
+    share = rows.shape[0]
+    rows = rows[None]
     bit = devices // 2
     while bit:
         other = exchange(rows, bit, devices)
         upper = my_bit(bit)
         rows = jnp.concatenate(
-            [jnp.where(upper, other, rows), jnp.where(upper, rows, other)], axis=0
-        )
+            [jnp.where(upper, other, rows), jnp.where(upper, rows, other)], axis=1
+        ).reshape(-1, share, D)
         bit = bit // 2
-    return rows
+    return rows.reshape(-1, D)
 
 
 def reduce_halves(values, devices):
     bit = 1
     while bit < devices:
-        half = values.shape[0] // 2
+        values = values.reshape(values.shape[0] // 2, 2, *values.shape[1:])
         upper = my_bit(bit)
-        low_part = values[:half]
-        high_part = values[half:]
-        keep = jnp.where(upper, high_part, low_part).astype(jnp.float32)
-        sent = jnp.where(upper, low_part, high_part)
+        keep = jnp.where(upper, values[:, 1], values[:, 0]).astype(jnp.float32)
+        sent = jnp.where(upper, values[:, 0], values[:, 1])
         values = (keep + exchange(sent, bit, devices).astype(jnp.float32)).astype(values.dtype)
         bit = bit * 2
-    return values
-
-
-def reverse_bits(count):
-    width = count.bit_length() - 1
-    return [int(format(i, "b").zfill(width)[::-1], 2) for i in range(count)]
+    return values[0]
 
 
 def all_to_all(values):
@@ -304,11 +299,41 @@
     return (rows_of(all_to_all(homed.reshape(devices, -1, piece))), small_all)
 
 
-def route_out(rows, place, slots, devices):
-    pieces = all_to_all(pieces_of(rows, devices)).reshape(place.shape[0], -1)
-    chosen = place[:, None] == jnp.arange(slots, dtype=jnp.int32)[None, :]
+def assemble_kernel(pieces_ref, out_ref, lines, columns):
+    devices, slots, _ = pieces_ref.shape
+    wide = D // devices
+    for row in range(BLOCK_ROWS):
+        for piece in range(devices):
+            lines[row * slots : (row + 1) * slots, piece * wide : (piece + 1) * wide] = pieces_ref[
+                piece, :, row * wide : (row + 1) * wide
+            ].astype(jnp.float32)
+    for group in range(D // PAIR):
+        lanes = slice(group * PAIR, (group + 1) * PAIR)
+        for row in range(BLOCK_ROWS):
+            columns[group, pl.ds(row, slots, stride=BLOCK_ROWS), :] = lines[
+                row * slots : (row + 1) * slots, lanes
+            ]
+        out_ref[:, lanes] = columns[group]
+
+
+def assemble(pieces):
+    rows = pieces.shape[1] * BLOCK_ROWS
+    return pl.pallas_call(
+        assemble_kernel,
+        out_shape=jax.ShapeDtypeStruct((rows, D), jnp.float32),
+        scratch_shapes=[
+            pltpu.VMEM((rows, D), jnp.float32),
+            pltpu.VMEM((D // PAIR, rows, PAIR), jnp.float32),
+        ],
+        name="assemble",
+    )(pieces)
+
+
+def route_out(columns, slot, slots, devices):
+    pieces = columns.T.reshape(slot.shape[0], -1)
+    chosen = slot[:, None] == jnp.arange(slots, dtype=jnp.int32)[None, :]
     slotted = inner_rows(chosen.astype(jnp.bfloat16), pieces).astype(jnp.bfloat16)
-    return rows_of(all_to_all(slotted.reshape(devices, -1, pieces.shape[1])))
+    return assemble(all_to_all(slotted.reshape(devices, -1, pieces.shape[1])))
 
 
 KEY_BLOCKS = D // BLOCK_ROWS
@@ -316,16 +341,6 @@
 
 def even_homes(blocks, devices):
     return KEY_BLOCKS % devices == 0 and (blocks - 2 * KEY_BLOCKS) % devices == 0
-
-
-def home_order(slot, devices, turned_groups):
-    order = jnp.array(reverse_bits(devices), dtype=jnp.int32)
-    parts = []
-    for group in range(turned_groups):
-        part = slot[group * KEY_BLOCKS : (group + 1) * KEY_BLOCKS]
-        parts.append(part.reshape(devices, -1)[order])
-    parts.append(slot[turned_groups * KEY_BLOCKS :].reshape(devices, -1))
-    return jnp.concatenate(parts, axis=1).reshape(-1)
 
 
 def gather_rows(weights, small, slot, devices):
@@ -335,34 +350,45 @@
     if not even_homes(slot.shape[0], devices):
         rows = unpack_rows(lax.all_gather(low, AXES, axis=0, tiled=True), slot)
         return (rows, lax.all_gather(small, AXES, axis=0, tiled=True))
-    homed, small_all = route_in(low, small, home_order(slot, devices, 1), slots, devices)
-    share = D // devices
-    rest = lax.all_gather(homed[share:], AXES, axis=0, tiled=True)
-    keys = gather_doubling(homed[:share], devices)
+    place = jnp.concatenate(
+        [slot[KEY_BLOCKS:].reshape(devices, -1), slot[:KEY_BLOCKS].reshape(devices, -1)], axis=1
+    ).reshape(-1)
+    homed, small_all = route_in(low, small, place, slots, devices)
+    split = homed.shape[0] - D // devices
+    rest = lax.all_gather(homed[:split], AXES, axis=0, tiled=True)
+    keys = gather_doubling(homed[split:], devices)
     return ((keys, rest[:D], rest[D : D + FF], rest[D + FF :]), small_all)
 
 
-def weight_grads_kernel(pre_ref, hidden_ref, active_ref, branch_ref, out_ref):
+def weight_grads_kernel(pre_ref, hidden_ref, active_ref, branch_ref, out_ref, turned):
     step = pl.program_id(0)
     half = pl.num_programs(0) // 2
 
+    @pl.when(step == 0)
+    def _():
+        turned[...] = hidden_ref[...].T
+
+    @pl.when(step == half)
+    def _():
+        turned[...] = branch_ref[...].T
+
     @pl.when(step < half)
     def _():
-        out_ref[...] = inner_rows(pre_ref[...], hidden_ref[...]).astype(jnp.bfloat16)
+        out_ref[...] = product(turned[...], pre_ref[...]).astype(jnp.bfloat16)
 
     @pl.when(step >= half)
     def _():
-        out_ref[...] = inner_rows(active_ref[...], branch_ref[...]).astype(jnp.bfloat16)
+        out_ref[...] = product(turned[...], active_ref[...]).astype(jnp.bfloat16)
 
 
 def weight_grads(grad_pre, hidden_low, active, grad_branch):
     rows = grad_pre.shape[0]
-    width = 512
+    width = 1024
     half = FF // width
     whole = pl.BlockSpec((rows, D), lambda i: (0, 0))
     return pl.pallas_call(
         weight_grads_kernel,
-        out_shape=jax.ShapeDtypeStruct((2 * FF, D), jnp.bfloat16),
+        out_shape=jax.ShapeDtypeStruct((D, 2 * FF), jnp.bfloat16),
         grid=(2 * half,),
         in_specs=[
             pl.BlockSpec((rows, width), lambda i: (0, jnp.minimum(i, half - 1))),
@@ -370,7 +396,8 @@
             pl.BlockSpec((rows, width), lambda i: (0, jnp.maximum(i - half, 0))),
             whole,
         ],
-        out_specs=pl.BlockSpec((width, D), lambda i: (i, 0)),
+        out_specs=pl.BlockSpec((D, width), lambda i: (0, i)),
+        scratch_shapes=[pltpu.VMEM((D, rows), jnp.bfloat16)],
         name="weight_grads",
     )(grad_pre, hidden_low, active, grad_branch)
 
@@ -378,7 +405,7 @@
 def scatter_grads(grad_key, grad_out, grad_wide, small_grad, slot, slots, devices):
     blocks = slot.shape[0]
     if not even_homes(blocks, devices):
-        rows = jnp.concatenate([grad_key, grad_out, grad_wide], axis=0)
+        rows = jnp.concatenate([grad_key, grad_out, grad_wide], axis=1).T
         rows = rows.reshape(blocks, BLOCK_ROWS * D)
         chosen = slot[:, None] == jnp.arange(slots, dtype=jnp.int32)[None, :]
         slotted = inner_rows(chosen.astype(jnp.bfloat16), rows).astype(jnp.bfloat16)
@@ -386,27 +413,23 @@
             lax.psum_scatter(slotted.reshape(-1, D), AXES, scatter_dimension=0, tiled=True),
             lax.psum_scatter(small_grad, AXES, scatter_dimension=0, tiled=True),
         )
-    wide_home = lax.psum_scatter(grad_wide, AXES, scatter_dimension=0, tiled=True)
-    order = jnp.array(reverse_bits(devices), dtype=jnp.int32)
+    wide_part = lax.psum_scatter(grad_wide, AXES, scatter_dimension=0, tiled=True)
     share = D // devices
     small_share = small_grad.shape[0] // devices
     small_deep = -(-small_share // D)
-    deep = -(-(2 * share + small_deep) // 8) * 8
-    small_rows = small_grad.reshape(devices, small_share)[order].astype(jnp.bfloat16)
+    deep = -(-(2 * share + small_deep) // 8) * 8 - 2 * share
     small_rows = jnp.pad(
-        small_rows, ((0, 0), (0, (deep - 2 * share) * D - small_share))
-    ).reshape(devices, -1, D)
+        small_grad.reshape(devices, small_share).astype(jnp.bfloat16),
+        ((0, 0), (0, deep * D - small_share)),
+    ).reshape(devices, deep, D)
     packed = jnp.concatenate(
         [grad_key.reshape(devices, share, D), grad_out.reshape(devices, share, D), small_rows],
         axis=1,
     )
-    summed = reduce_halves(packed.reshape(-1, D), devices)
-    home = jnp.concatenate([summed[: 2 * share], wide_home], axis=0)
-    small_home = summed[2 * share : 2 * share + small_deep].reshape(-1)[:small_share]
-    return (
-        route_out(home, home_order(slot, devices, 2), slots, devices).astype(jnp.float32),
-        small_home.astype(jnp.float32),
-    )
+    summed = reduce_halves(packed, devices)
+    columns = jnp.concatenate([summed[:share], summed[share : 2 * share], wide_part], axis=1)
+    small_part = summed[2 * share : 2 * share + small_deep].reshape(-1)[:small_share]
+    return (route_out(columns, slot, slots, devices), small_part.astype(jnp.float32))
 
 
 def adamw_update(master, first, second, grad, decay, rate):
@@ -494,12 +517,12 @@
     grad_first = norm_back(grad_hidden * gain_one, norm_one, inverse_one)
     grad_attended = grad_first.astype(jnp.bfloat16)
     grad_out_bias = jnp.sum(grad_attended.astype(jnp.float32), axis=0)
-    grad_out = inner_rows(context, grad_attended).astype(jnp.bfloat16)
+    grad_out = inner_rows(grad_attended, context).astype(jnp.bfloat16)
     grad_context = product_t(grad_attended, out_rows).astype(jnp.bfloat16)
     grad_query, grad_keys, grad_values = attend_backward(
         spans, query, keys, values, context, grad_context, log_total
     )
-    grad_key = inner_rows(hidden_in, grad_keys).astype(jnp.bfloat16)
+    grad_key = inner_rows(grad_keys, hidden_in).astype(jnp.bfloat16)
     grad_query_wide = grad_query.astype(jnp.float32)
     grad_values_wide = grad_values.astype(jnp.float32)
     grad_scale_q_out = jnp.sum(grad_query_wide * side_q, axis=0)

time: 453 us -> 429 us (0.947)
  waiting for transfers between devices: 159 us -> 148 us
  starting transfers between devices: 25.6 us -> 18.4 us
  local copies, waits for them, and re-layouts: 31.8 us -> 25.3 us
    all_to_all x3 -> x2, waiting for transfers between devices: 49.2 us -> 42.8 us  [all_to_all(): return lax.all_to_all(values, AXES, split_axis=0, concat_axis=0, tiled=True)]
    all_to_all x3 -> x2, starting transfers between devices: 14.6 us -> 11.2 us  [all_to_all(): return lax.all_to_all(values, AXES, split_axis=0, concat_axis=0, tiled=True)]
    pallas_call x1 -> x2, Pallas kernels: 18.6 us -> 20.7 us  [the longest x1 16.9 us: weight_grads(): pl.pallas_call(weight_grads_kernel, out_shape=jax.ShapeDtypeStruct((D, 2...]
  transfers between devices with their start and end apart: 15 -> 14, of which waited for: 14 -> 13; matrix products, arithmetic and copies ran while one was open for 17% -> 17% of each run, Pallas kernels for 13% -> 13%
where the time goes in v3:
time: 429 us; the launch traced here: 423 us
  waiting for transfers between devices  148 us (34%)
  matrix products  93.9 us (22%)
  Pallas kernels  77.5 us (18%)
  local copies, waits for them, and re-layouts  25.3 us (6%)
  other arithmetic  24.6 us (6%)
  blocking collectives  20.4 us (5%)
  starting transfers between devices  18.4 us (4%)
  between operations  15.1 us (4%)
    ppermute x10, waiting for transfers between devices, exchange(): return lax.ppermute(values, AXES, [(i, i ^ bit) for i in range(devices)])  67.7 us
    dot_general x9, matrix products, product_t(): lax.dot_general(left, right, (((1,), (1,)), ((), ())), preferred_element_...  45 us
    all_to_all x2, waiting for transfers between devices, all_to_all(): return lax.all_to_all(values, AXES, split_axis=0, concat_axis=0, tiled=True)  42.8 us
    dot_general x10, matrix products, product(): return jnp.dot(left, right, preferred_element_type=jnp.float32)  40.9 us
    pallas_call x1, Pallas kernels, attend_backward(): pl.pallas_call(attend_backward_kernel, out_shape=(shape, shape, shape), g...  34.4 us
    all_gather x1, waiting for transfers between devices, gather_rows(): rest = lax.all_gather(homed[:split], AXES, axis=0, tiled=True)  23.4 us
    pallas_call x1, Pallas kernels, attend_forward(): pl.pallas_call(attend_forward_kernel, out_shape=(jax.ShapeDtypeStruct((ro...  22.4 us
    all_to_all x1, blocking collectives, all_to_all(): return lax.all_to_all(values, AXES, split_axis=0, concat_axis=0, tiled=True)  20.4 us
  transfers between devices with their start and end apart: 14, of which 13 were waited for; matrix products, arithmetic and copies ran while one was open for 17% of the time, Pallas kernels for 13%

profile of v3, /device:TPU:0, one launch (start us, length us, event | category | flops | bytes accessed | tf_op | source)
XLA Modules:
  0.0 423.4 jit_solution(4063096553683944906)
XLA Ops:
  12.0 7.3 %all-to-all-start = ((bf16[32,42,288]{2,1,0:T(8,128)(2,1)}), bf16[32,42,288]{2,1,0:T(8,128)(2,1)S(1)}, u32[]{:S(2)}, u32[]{:S(2)}) async-start(bf16[32,42,288]{2,1,0:T(8,128)(2,1)} %pad_maximum_fusion.1), calls=%async_computation | async-start | bytes 2359296 | tf_op jit(solution)/shard_map/all_to_all | solution.py:277
  20.2 28.2 %all-to-all-done = bf16[32,42,288]{2,1,0:T(8,128)(2,1)S(1)} async-done(((bf16[32,42,288]{2,1,0:T(8,128)(2,1)}), bf16[32,42,288]{2,1,0:T(8,128)(2,1)S(1)}, u32[]{:S(2)}, u32[]{:S(2)}) %all-to-all-start) | async-done | bytes 774176 | tf_op jit(solution)/shard_map/all_to_all | solution.py:277
  52.4 20.4 %all_to_all.15 = bf16[32,20,288]{2,1,0:T(8,128)(2,1)S(1)} all-to-all(bf16[32,20,288]{2,1,0:T(8,128)(2,1)} %reshape.237), channel_id=1, replica_groups=mesh['rows'=8,'heads'=4] {'rows','heads'}, dimensions={0} | all-to-all | bytes 737280 | tf_op jit(solution)/shard_map/all_to_all | solution.py:277
  78.6 5.0 %convolution_convert_fusion = bf16[1024,1024]{1,0:T(8,128)(2,1)} fusion(bf16[1024,768]{1,0:T(8,128)(2,1)} %param.15, bf16[768,1024]{1,0:T(8,128)(2,1)} %param.21), kind=kOutput, calls=%fused_computation.75 | convolution fusion | flops 1611661312 | bytes 5242880 | tf_op jit(solution)/shard_map/dot_general | solution.py:42
  91.6 5.0 %collective-permute-done.1 = bf16[2,24,768]{2,1,0:T(8,128)(2,1)S(1)} collective-permute-done((bf16[2,24,768]{2,1,0:T(8,128)(2,1)S(1)}, bf16[2,24,768]{2,1,0:T(8,128)(2,1)S(1)}, u32[]{:S(2)}, u32[]{:S(2)}) %collective-permute-start.1) | collective-permute-done | bytes 73760 | tf_op jit(solution)/shard_map/ppermute | solution.py:243
  105.2 8.5 %collective-permute-done.3 = bf16[8,24,768]{2,1,0:T(8,128)(2,1)S(1)} collective-permute-done((bf16[8,24,768]{2,1,0:T(8,128)(2,1)S(1)}, bf16[8,24,768]{2,1,0:T(8,128)(2,1)S(1)}, u32[]{:S(2)}, u32[]{:S(2)}) %collective-permute-start.3) | collective-permute-done | bytes 294944 | tf_op jit(solution)/shard_map/ppermute | solution.py:243
  120.2 22.4 %attend_forward.1 = (bf16[1024,768]{1,0:T(8,128)(2,1)}, f32[6,2,1024]{2,1,0:T(2,128)}) custom-call(s32[3]{0:T(128)} %pad_add_fusion.1.spans, bf16[1024,768]{1,0:T(8,128)(2,1)} %add_convert_fusion.4.query_ref, bf16[1024,768]{1,0:T(8,128)(2,1)} %fusion.55.keys_ref, bf16[1024,768]{1,0:T(8,128)(2,1)} %add_convert_fusion.3.values_ref), custom_call_target="tpu_custom_call" | custom-call | tf_op jit(solution)/shard_map/attend_forward/pallas_call | solution.py:199
  142.6 23.4 %all-gather.2.cloned.1.call-done = bf16[6912,768]{1,0:T(8,128)(2,1)} async-done(((bf16[216,768]{1,0:T(8,128)(2,1)}), bf16[6912,768]{1,0:T(8,128)(2,1)}) %all-gather.2.cloned.1.call-update) | async-done | bytes 10616848 | tf_op jit(solution)/shard_map/all_gather | solution.py:358
  166.0 3.9 fusion.80
  172.3 11.9 %fusion.4 = (bf16[1024,3072]{1,0:T(8,128)(2,1)S(1)}, bf16[1024,3072]{1,0:T(8,128)(2,1)S(1)}) fusion(f32[3072]{0:T(1024)S(1)} %slice_convert_fusion, bf16[1024,768]{1,0:T(8,128)(2,1)S(1)} %fusion.29.hidden_ref, bf16[6912,768]{1,0:T(8,128)(2,1)S(1)} %copy-done.36), kind=kOutput, calls=%fused_computation.5 | convolution fusion | flops 4869586944 | bytes 18886656 | tf_op jit(solution)/shard_map/dot_general | solution.py:46
  184.2 5.4 %fusion.81 = (f32[1024]{0:T(1024)S(1)}, f32[1024,768]{1,0:T(8,128)S(1)}) fusion(f32[768]{0:T(1024)S(1)} %get-tuple-element.63, bf16[1024,3072]{1,0:T(8,128)(2,1)S(1)} %get-tuple-element.18.active_ref, bf16[6912,768]{1,0:T(8,128)(2,1)S(1)} %copy-done.36, f32[768]{0:T(1024)S(1)} %get-tuple-element.64, f32[768]{0:T(1024)S(1)} %get-tuple-element.65, ...), kind=kOutput, calls=%fused_computation.179 | convolution fusion | flops 4837342208 | bytes 17326080 | tf_op jit(solution)/shard_map/dot_general | solution.py:42
  196.6 7.1 %fusion.82 = (bf16[3072]{0:T(1024)(128)(2,1)S(1)}, bf16[1024,3072]{1,0:T(8,128)(2,1)}) fusion(bf16[1024,3072]{1,0:T(8,128)(2,1)S(1)} %get-tuple-element.19, bf16[1024,768]{1,0:T(8,128)(2,1)S(1)} %get-tuple-element.42.branch_ref, bf16[6912,768]{1,0:T(8,128)(2,1)S(1)} %copy-done.36), kind=kOutput, calls=%fused_computation.180 | convolution fusion | flops 4844418048 | bytes 18880512 | tf_op jit(solution)/shard_map/dot_general | solution.py:46
  203.6 16.9 %weight_grads.1 = bf16[768,6144]{1,0:T(8,128)(2,1)} custom-call(bf16[1024,3072]{1,0:T(8,128)(2,1)} %get-tuple-element.78.pre_ref, bf16[1024,768]{1,0:T(8,128)(2,1)} %copy-done.11, bf16[1024,3072]{1,0:T(8,128)(2,1)} %copy-done.13, bf16[1024,768]{1,0:T(8,128)(2,1)} %copy-done.12), custom_call_target="tpu_custom_call" | custom-call | tf_op jit(solution)/shard_map/weight_grads/pallas_call | solution.py:389
  220.6 11.7 %multiply_reduce_fusion = (bf16[768]{0:T(1024)(128)(2,1)S(1)}, f32[1024]{0:T(1024)S(1)}, f32[1024]{0:T(1024)S(1)}, bf16[768]{0:T(1024)(128)(2,1)S(1)}, f32[1024,768]{1,0:T(8,128)S(1)}) fusion(f32[1024,768]{1,0:T(8,128)} %copy-done.2, f32[1024]{0:T(1024)S(1)} %add_rsqrt_fusion.1, f32[1024]{0:T(1024)S(1)} %broadcast_multiply_fusion.5, ...), kind=kOutput, calls=%fused_computation.46 | convolution fusion | flops 4845989888 | bytes 22062080 | tf_op jit(solution)/shard_map/dot_general | solution.py:42
  233.4 4.8 %convolution_convert_fusion.2.grad_ref = bf16[1024,768]{1,0:T(8,128)(2,1)} fusion(bf16[6912,768]{1,0:T(8,128)(2,1)} %all-gather.2.cloned.1.call-done, f32[1024,768]{1,0:T(8,128)S(1)} %get-tuple-element.44), kind=kOutput, calls=%fused_computation.78 | convolution fusion | flops 1209532416 | bytes 5898240 | tf_op jit(solution)/shard_map/dot_general | solution.py:46
  238.3 34.4 %attend_backward.1 = (bf16[1024,768]{1,0:T(8,128)(2,1)}, bf16[1024,768]{1,0:T(8,128)(2,1)}, bf16[1024,768]{1,0:T(8,128)(2,1)}) custom-call(s32[3]{0:T(128)} %pad_add_fusion.1.spans, bf16[1024,768]{1,0:T(8,128)(2,1)} %add_convert_fusion.4.query_ref, bf16[1024,768]{1,0:T(8,128)(2,1)} %fusion.55.keys_ref, bf16[1024,768]{1,0:T(8,128)(2,1)} %add_convert_fusion.3.values_ref, ...), custom_call_target="tpu_custom_call" | custom-call | tf_op jit(solution)/shard_map/attend_backward/pallas_call | solution.py:221
  276.1 4.1 fusion.8
  297.5 22.0 %collective-permute-done.6 = bf16[8,56,768]{2,1,0:T(8,128)(2,1)S(1)} collective-permute-done((bf16[8,56,768]{2,1,0:T(8,128)(2,1)S(1)}, bf16[8,56,768]{2,1,0:T(8,128)(2,1)S(1)}, u32[]{:S(2)}, u32[]{:S(2)}) %collective-permute-start.6) | collective-permute-done | bytes 688160 | tf_op jit(solution)/shard_map/ppermute | solution.py:243
  321.3 15.0 %collective-permute-done.7 = bf16[4,56,768]{2,1,0:T(8,128)(2,1)S(1)} collective-permute-done((bf16[4,56,768]{2,1,0:T(8,128)(2,1)S(1)}, bf16[4,56,768]{2,1,0:T(8,128)(2,1)S(1)}, u32[]{:S(2)}, u32[]{:S(2)}) %collective-permute-start.7) | collective-permute-done | bytes 344096 | tf_op jit(solution)/shard_map/ppermute | solution.py:243
  340.1 7.5 %collective-permute-done.8 = bf16[2,56,768]{2,1,0:T(8,128)(2,1)S(1)} collective-permute-done((bf16[2,56,768]{2,1,0:T(8,128)(2,1)S(1)}, bf16[2,56,768]{2,1,0:T(8,128)(2,1)S(1)}, u32[]{:S(2)}, u32[]{:S(2)}) %collective-permute-start.8) | collective-permute-done | bytes 172064 | tf_op jit(solution)/shard_map/ppermute | solution.py:243
  353.9 14.2 %reduce-scatter.2.cloned.1.call-done = bf16[24,6144]{1,0:T(8,128)(2,1)} async-done(((bf16[768,6144]{1,0:T(8,128)(2,1)}), bf16[24,6144]{1,0:T(8,128)(2,1)}) %reduce-scatter.2.cloned.1.call-update) | async-done | bytes 294928 | tf_op jit(solution)/shard_map/reduce_scatter | solution.py:416
  386.9 4.2 %add_convert_fusion.1 = bf16[1024,768]{1,0:T(8,128)(2,1)} fusion(f32[1024,768]{1,0:T(8,128)S(1)} %copy-done.10, f32[1024,768]{1,0:T(8,128)S(1)} %fusion.84, f32[1024,768]{1,0:T(8,128)S(1)} %copy-done.9, f32[1024,768]{1,0:T(8,128)S(1)} %copy-done.20, bf16[1024,768]{1,0:T(8,128)(2,1)} %get-tuple-element.22, bf16[768,768]{1,0:T(8,128)(2,1)S(1)} %bitcast.145), kind=kOutput, calls=%fused_computation.47 | convolution fusion | flops 1211891712 | bytes 16908288 | tf_op jit(solution)/shard_map/dot_general | solution.py:46
  392.6 14.6 %all-to-all-done.2.pieces_ref = bf16[32,40,288]{2,1,0:T(8,128)(2,1)} async-done(((bf16[32,40,288]{2,1,0:T(8,128)(2,1)}), bf16[32,40,288]{2,1,0:T(8,128)(2,1)}, u32[]{:S(2)}, u32[]{:S(2)}) %all-to-all-start.2) | async-done | bytes 737312 | tf_op jit(solution)/shard_map/all_to_all | solution.py:277
  411.0 5.4 %fusion.76 = (bf16[480,768]{1,0:T(8,128)(2,1)}, f32[480,768]{1,0:T(8,128)}, f32[480,768]{1,0:T(8,128)}, f32[480,768]{1,0:T(8,128)}) fusion(f32[480,768]{1,0:T(8,128)S(1)} %copy-done.17, f32[480,768]{1,0:T(8,128)} %assemble.1, f32[480,768]{1,0:T(8,128)} %param.25, f32[480,768]{1,0:T(8,128)} %param.26), kind=kLoop, calls=%fused_computation.176 | loop fusion | flops 5529600 | bytes 11059200 | tf_op jit(solution)/shard_map/convert_element_type | solution.py:572
  (209 shorter events, 105.0 us)
Async XLA Ops:
  7.2 77.4 %copy-start = (bf16[1024,768]{1,0:T(8,128)(2,1)S(1)}, bf16[1024,768]{1,0:T(8,128)(2,1)}, u32[]{:S(2)}) copy-start(bf16[1024,768]{1,0:T(8,128)(2,1)} %param.22) | copy-start | bytes 4718596
  12.0 36.3 %all-to-all-start = ((bf16[32,42,288]{2,1,0:T(8,128)(2,1)}), bf16[32,42,288]{2,1,0:T(8,128)(2,1)S(1)}, u32[]{:S(2)}, u32[]{:S(2)}) async-start(bf16[32,42,288]{2,1,0:T(8,128)(2,1)} %pad_maximum_fusion.1), calls=%async_computation | async-start | bytes 2359296 | tf_op jit(solution)/shard_map/all_to_all | solution.py:277
  19.3 146.7 %all-gather.2.cloned.1.call-start = ((), (), s32[]{:S(2)}) async-start(), calls=%async_computation.4 | async-start | bytes 10948608 | tf_op jit(solution)/shard_map/all_gather | solution.py:358
  50.2 26.3 %copy-start.35 = (s32[4,2]{0,1:T(2,128)S(1)}, s32[4,2]{0,1:T(2,128)}, u32[]{:S(2)}) copy-start(s32[4,2]{0,1:T(2,128)} %param.17) | copy-start | bytes 100
  50.2 26.5 %copy-start.41 = (s32[4]{0:T(128)S(1)}, s32[4]{0:T(128)}, u32[]{:S(2)}) copy-start(s32[4]{0:T(128)} %param.18) | copy-start | bytes 52
  76.2 291.8 %reduce-scatter.2.cloned.1.call-start = ((), (), s32[]{:S(2)}) async-start(), calls=%async_computation.5 | async-start | bytes 9732096 | tf_op jit(solution)/shard_map/reduce_scatter | solution.py:416
  84.1 7.4 %collective-permute-start = (bf16[1,24,768]{2,1,0:T(8,128)(2,1)S(1)}, bf16[1,24,768]{2,1,0:T(8,128)(2,1)S(1)}, u32[]{:S(2)}, u32[]{:S(2)}) collective-permute-start(bf16[1,24,768]{2,1,0:T(8,128)(2,1)S(1)} %broadcast_in_dim.8), channel_id=1, source_target_pairs={{0,16},{1,17},{2,18},{3,19},{4,20},{5,21},{6,22},{7,23},{8,24},{9,... | collective-permute-start | bytes 110600 | tf_op jit(solution)/shard_map/ppermute | solution.py:243
  84.6 13.4 %copy-start.37 = (bf16[1024,768]{1,0:T(8,128)(2,1)S(1)}, bf16[1024,768]{1,0:T(8,128)(2,1)}, u32[]{:S(2)}) copy-start(bf16[1024,768]{1,0:T(8,128)(2,1)} %param.15) | copy-start | bytes 4718596
  84.6 13.4 %copy-start.40 = (bf16[768,768]{1,0:T(8,128)(2,1)S(1)}, bf16[768,768]{1,0:T(8,128)(2,1)}, u32[]{:S(2)}) copy-start(bf16[768,768]{1,0:T(8,128)(2,1)} %param.20) | copy-start | bytes 3538948
  91.5 5.1 %collective-permute-start.1 = (bf16[2,24,768]{2,1,0:T(8,128)(2,1)S(1)}, bf16[2,24,768]{2,1,0:T(8,128)(2,1)S(1)}, u32[]{:S(2)}, u32[]{:S(2)}) collective-permute-start(bf16[2,24,768]{2,1,0:T(8,128)(2,1)S(1)} %bitcast.163), channel_id=1, source_target_pairs={{0,8},{1,9},{2,10},{3,11},{4,12},{5,13},{6,14},{7,15},{8,0},{9,1},... | collective-permute-start | bytes 221192 | tf_op jit(solution)/shard_map/ppermute | solution.py:243
  96.7 5.2 %collective-permute-start.2 = (bf16[4,24,768]{2,1,0:T(8,128)(2,1)S(1)}, bf16[4,24,768]{2,1,0:T(8,128)(2,1)S(1)}, u32[]{:S(2)}, u32[]{:S(2)}) collective-permute-start(bf16[4,24,768]{2,1,0:T(8,128)(2,1)S(1)} %bitcast.161), channel_id=1, source_target_pairs={{0,4},{1,5},{2,6},{3,7},{4,0},{5,1},{6,2},{7,3},{8,12},{9,13},{10,... | collective-permute-start | bytes 442376 | tf_op jit(solution)/shard_map/ppermute | solution.py:243
  101.9 11.8 %collective-permute-start.3 = (bf16[8,24,768]{2,1,0:T(8,128)(2,1)S(1)}, bf16[8,24,768]{2,1,0:T(8,128)(2,1)S(1)}, u32[]{:S(2)}, u32[]{:S(2)}) collective-permute-start(bf16[8,24,768]{2,1,0:T(8,128)(2,1)S(1)} %bitcast.156), channel_id=1, source_target_pairs={{0,2},{1,3},{2,0},{3,1},{4,6},{5,7},{6,4},{7,5},{8,10},{9,11},{10,... | collective-permute-start | bytes 884744 | tf_op jit(solution)/shard_map/ppermute | solution.py:243
  113.8 2.7 collective-permute-start.4
  170.0 14.2 %copy-start.2 = (f32[1024,768]{1,0:T(8,128)}, f32[1024,768]{1,0:T(8,128)S(1)}, u32[]{:S(2)}) copy-start(f32[1024,768]{1,0:T(8,128)S(1)} %get-tuple-element.72) | copy-start | bytes 9437188
  292.2 3.2 collective-permute-start.5
  295.4 41.2 %copy-start.6 = (f32[1024,1024]{1,0:T(8,128)S(1)}, f32[1024,1024]{1,0:T(8,128)}, u32[]{:S(2)}) copy-start(f32[1024,1024]{1,0:T(8,128)} %get-tuple-element.76) | copy-start | bytes 12582916
  296.0 40.6 %copy-start.28 = (bf16[768,1024]{1,0:T(8,128)(2,1)S(1)}, bf16[768,1024]{1,0:T(8,128)(2,1)}, u32[]{:S(2)}) copy-start(bf16[768,1024]{1,0:T(8,128)(2,1)} %param.21) | copy-start | bytes 4718596
  296.1 40.5 %copy-start.5 = (f32[1024,1024]{1,0:T(8,128)S(1)}, f32[1024,1024]{1,0:T(8,128)}, u32[]{:S(2)}) copy-start(f32[1024,1024]{1,0:T(8,128)} %copy-done.4) | copy-start | bytes 12582916
  296.1 23.4 %collective-permute-start.6 = (bf16[8,56,768]{2,1,0:T(8,128)(2,1)S(1)}, bf16[8,56,768]{2,1,0:T(8,128)(2,1)S(1)}, u32[]{:S(2)}, u32[]{:S(2)}) collective-permute-start(bf16[8,56,768]{2,1,0:T(8,128)(2,1)S(1)} %fusion.61), channel_id=1, source_target_pairs={{0,2},{1,3},{2,0},{3,1},{4,6},{5,7},{6,4},{7,5},{8,10},{9,11},{10,... | collective-permute-start | bytes 2064392 | tf_op jit(solution)/shard_map/ppermute | solution.py:243
  319.8 16.5 %collective-permute-start.7 = (bf16[4,56,768]{2,1,0:T(8,128)(2,1)S(1)}, bf16[4,56,768]{2,1,0:T(8,128)(2,1)S(1)}, u32[]{:S(2)}, u32[]{:S(2)}) collective-permute-start(bf16[4,56,768]{2,1,0:T(8,128)(2,1)S(1)} %fusion.64), channel_id=1, source_target_pairs={{0,4},{1,5},{2,6},{3,7},{4,0},{5,1},{6,2},{7,3},{8,12},{9,13},{10,... | collective-permute-start | bytes 1032200 | tf_op jit(solution)/shard_map/ppermute | solution.py:243
  336.5 11.2 %collective-permute-start.8 = (bf16[2,56,768]{2,1,0:T(8,128)(2,1)S(1)}, bf16[2,56,768]{2,1,0:T(8,128)(2,1)S(1)}, u32[]{:S(2)}, u32[]{:S(2)}) collective-permute-start(bf16[2,56,768]{2,1,0:T(8,128)(2,1)S(1)} %select_bitcast_fusion.1), channel_id=1, source_target_pairs={{0,8},{1,9},{2,10},{3,11},{4,12},{5,13},{6,14},{7,15},{8,0},{9,1},... | collective-permute-start | bytes 516104 | tf_op jit(solution)/shard_map/ppermute | solution.py:243
  347.7 5.4 %collective-permute-start.9 = (bf16[1,56,768]{2,1,0:T(8,128)(2,1)S(1)}, bf16[1,56,768]{2,1,0:T(8,128)(2,1)S(1)}, u32[]{:S(2)}, u32[]{:S(2)}) collective-permute-start(bf16[1,56,768]{2,1,0:T(8,128)(2,1)S(1)} %select_bitcast_fusion.2), channel_id=1, source_target_pairs={{0,16},{1,17},{2,18},{3,19},{4,20},{5,21},{6,22},{7,23},{8,24},{9,... | collective-permute-start | bytes 258056 | tf_op jit(solution)/shard_map/ppermute | solution.py:243
  378.6 28.6 %all-to-all-start.2 = ((bf16[32,40,288]{2,1,0:T(8,128)(2,1)}), bf16[32,40,288]{2,1,0:T(8,128)(2,1)}, u32[]{:S(2)}, u32[]{:S(2)}) async-start(bf16[32,40,288]{2,1,0:T(8,128)(2,1)} %bitcast.146), calls=%async_computation.3 | async-start | bytes 1966080 | tf_op jit(solution)/shard_map/all_to_all | solution.py:277
  391.1 19.9 %copy-start.17 = (f32[480,768]{1,0:T(8,128)S(1)}, f32[480,768]{1,0:T(8,128)}, u32[]{:S(2)}) copy-start(f32[480,768]{1,0:T(8,128)} %param.24) | copy-start | bytes 4423684
  (32 other events, 192.5 us)
Sparse Core Ops, SparseCore 0:
  76.3 89.7 all-gather.1
  220.7 147.3 reduce-scatter.1

commit v4 on v3

--- a/solution.py
+++ b/solution.py
@@ -285,18 +285,38 @@
     return pieces.transpose(1, 0, 2).reshape(-1, D)
 
 
+def pick_kernel(place_ref, pieces_ref, out_ref):
+    blocks, piece = out_ref.shape
+    slots = pieces_ref.shape[0]
+    chosen = place_ref[...] == lax.broadcasted_iota(jnp.int32, (blocks, slots), 1)
+    chosen = jnp.where(chosen, 1.0, 0.0).astype(jnp.bfloat16)
+    out_ref[...] = product(chosen, pieces_ref[...])[:, :piece].astype(jnp.bfloat16)
+
+
+def pick(place, pieces, piece):
+    return pl.pallas_call(
+        pick_kernel,
+        out_shape=jax.ShapeDtypeStruct((place.shape[0], piece), jnp.bfloat16),
+        name="pick",
+    )(place[:, None], pieces)
+
+
+def spare_lanes(devices):
+    return -(BLOCK_ROWS * D // devices) % PAIR
+
+
 def route_in(rows, small, place, slots, devices):
     pieces = pieces_of(rows, devices)
-    piece = pieces.shape[2]
-    extra = -(-small.shape[0] // piece)
-    tail = jnp.pad(small, (0, extra * piece - small.shape[0])).reshape(1, extra, piece)
-    tail = jnp.broadcast_to(tail, (devices, extra, piece))
-    moved = all_to_all(jnp.concatenate([pieces, tail], axis=1))
-    small_all = moved[:, -extra:].reshape(devices, -1)[:, : small.shape[0]].reshape(-1)
-    pieces = moved[:, :-extra].reshape(slots, piece)
-    chosen = place[:, None] == jnp.arange(slots, dtype=jnp.int32)[None, :]
-    homed = product(chosen.astype(jnp.bfloat16), pieces).astype(jnp.bfloat16)
-    return (rows_of(all_to_all(homed.reshape(devices, -1, piece))), small_all)
+    _, capacity, piece = pieces.shape
+    spare = spare_lanes(devices)
+    deep = -(-small.shape[0] // spare)
+    tail = jnp.pad(small, (0, deep * spare - small.shape[0])).reshape(deep, spare)
+    tail = jnp.pad(tail, ((0, capacity - deep), (0, 0)))[None]
+    tail = jnp.broadcast_to(tail, (devices, capacity, spare))
+    moved = all_to_all(jnp.concatenate([pieces, tail], axis=2))
+    small_all = moved[:, :deep, piece:].reshape(devices, -1)[:, : small.shape[0]].reshape(-1)
+    homed = pick(place, moved.reshape(slots, -1), piece)
+    return (all_to_all(homed.reshape(devices, -1, piece)), small_all)
 
 
 def assemble_kernel(pieces_ref, out_ref, lines, columns):
@@ -329,34 +349,60 @@
     )(pieces)
 
 
-def route_out(columns, slot, slots, devices):
-    pieces = columns.T.reshape(slot.shape[0], -1)
-    chosen = slot[:, None] == jnp.arange(slots, dtype=jnp.int32)[None, :]
-    slotted = inner_rows(chosen.astype(jnp.bfloat16), pieces).astype(jnp.bfloat16)
-    return assemble(all_to_all(slotted.reshape(devices, -1, pieces.shape[1])))
+def place_kernel(wide_ref, narrow_ref, slot_ref, out_ref, turned, lined):
+    columns = wide_ref.shape[0]
+    slots = out_ref.shape[0]
+    blocks = lined.shape[0]
+    for group in range(2):
+        part = narrow_ref[group * columns : (group + 1) * columns, :]
+        turned[group * D : (group + 1) * D, :] = part.astype(jnp.float32).T
+    turned[2 * D :, :] = wide_ref[...].astype(jnp.float32).T
+    for row in range(BLOCK_ROWS):
+        lined[:, row * columns : (row + 1) * columns] = turned[
+            pl.ds(row, blocks, stride=BLOCK_ROWS), :
+        ]
+    chosen = slot_ref[...] == lax.broadcasted_iota(jnp.int32, (slots, blocks), 0)
+    chosen = jnp.where(chosen, 1.0, 0.0).astype(jnp.bfloat16)
+    out_ref[...] = product(chosen, lined[...].astype(jnp.bfloat16)).astype(jnp.bfloat16)
+
+
+def route_out(wide, narrow, slot, slots, devices):
+    columns = wide.shape[0]
+    blocks = slot.shape[0]
+    slotted = pl.pallas_call(
+        place_kernel,
+        out_shape=jax.ShapeDtypeStruct((slots, BLOCK_ROWS * columns), jnp.bfloat16),
+        scratch_shapes=[
+            pltpu.VMEM((blocks * BLOCK_ROWS, columns), jnp.float32),
+            pltpu.VMEM((blocks, BLOCK_ROWS * columns), jnp.float32),
+        ],
+        name="place",
+    )(wide, narrow, slot[None, :])
+    return assemble(all_to_all(slotted.reshape(devices, -1, BLOCK_ROWS * columns)))
 
 
 KEY_BLOCKS = D // BLOCK_ROWS
 
 
-def even_homes(blocks, devices):
-    return KEY_BLOCKS % devices == 0 and (blocks - 2 * KEY_BLOCKS) % devices == 0
+def even_homes(blocks, capacity, small_share, devices):
+    fits = spare_lanes(devices) * capacity >= small_share
+    return fits and KEY_BLOCKS % devices == 0 and (blocks - 2 * KEY_BLOCKS) % devices == 0
 
 
 def gather_rows(weights, small, slot, devices):
     slots = devices * (weights.shape[0] // BLOCK_ROWS)
     low = weights.astype(jnp.bfloat16)
     small = small.astype(jnp.bfloat16)
-    if not even_homes(slot.shape[0], devices):
+    if not even_homes(slot.shape[0], slots // devices, small.shape[0], devices):
         rows = unpack_rows(lax.all_gather(low, AXES, axis=0, tiled=True), slot)
         return (rows, lax.all_gather(small, AXES, axis=0, tiled=True))
     place = jnp.concatenate(
         [slot[KEY_BLOCKS:].reshape(devices, -1), slot[:KEY_BLOCKS].reshape(devices, -1)], axis=1
     ).reshape(-1)
     homed, small_all = route_in(low, small, place, slots, devices)
-    split = homed.shape[0] - D // devices
-    rest = lax.all_gather(homed[:split], AXES, axis=0, tiled=True)
-    keys = gather_doubling(homed[split:], devices)
+    split = homed.shape[1] - KEY_BLOCKS // devices
+    rest = lax.all_gather(rows_of(homed[:, :split]), AXES, axis=0, tiled=True)
+    keys = gather_doubling(rows_of(homed[:, split:]), devices)
     return ((keys, rest[:D], rest[D : D + FF], rest[D + FF :]), small_all)
 
 
@@ -404,7 +450,7 @@
 
 def scatter_grads(grad_key, grad_out, grad_wide, small_grad, slot, slots, devices):
     blocks = slot.shape[0]
-    if not even_homes(blocks, devices):
+    if not even_homes(blocks, slots // devices, small_grad.shape[0] // devices, devices):
         rows = jnp.concatenate([grad_key, grad_out, grad_wide], axis=1).T
         rows = rows.reshape(blocks, BLOCK_ROWS * D)
         chosen = slot[:, None] == jnp.arange(slots, dtype=jnp.int32)[None, :]
@@ -427,9 +473,8 @@
         axis=1,
     )
     summed = reduce_halves(packed, devices)
-    columns = jnp.concatenate([summed[:share], summed[share : 2 * share], wide_part], axis=1)
     small_part = summed[2 * share : 2 * share + small_deep].reshape(-1)[:small_share]
-    return (route_out(columns, slot, slots, devices), small_part.astype(jnp.float32))
+    return (route_out(wide_part, summed, slot, slots, devices), small_part.astype(jnp.float32))
 
 
 def adamw_update(master, first, second, grad, decay, rate):

time: 429 us -> 418 us (0.974)
  Pallas kernels: 77.5 us -> 84.8 us
  local copies, waits for them, and re-layouts: 25.3 us -> 19 us
  matrix products: 93.9 us -> 88.7 us
  waiting for transfers between devices: 148 us -> 143 us
    pallas_call x0 -> x2, Pallas kernels: none -> 7.55 us  [the longest x1 4.41 us: route_out(): pl.pallas_call(place_kernel, out_shape=jax.ShapeDtypeStruct((slots, BLOCK...]
    all_to_all x2, waiting for transfers between devices: 42.8 us -> 37.8 us  [all_to_all(): return lax.all_to_all(values, AXES, split_axis=0, concat_axis=0, tiled=True)]
    dot_general x10 -> x9, matrix products: 40.9 us -> 38.6 us  [product(): return jnp.dot(left, right, preferred_element_type=jnp.float32)]
  transfers between devices with their start and end apart: 14 -> 14, of which waited for: 13 -> 13; matrix products, arithmetic and copies ran while one was open for 17% -> 18% of each run, Pallas kernels for 13% -> 14%
where the time goes in v4:
time: 418 us; the launch traced here: 414 us
  waiting for transfers between devices  143 us (34%)
  matrix products  88.7 us (21%)
  Pallas kernels  84.8 us (20%)
  other arithmetic  23.8 us (6%)
  blocking collectives  20.2 us (5%)
  starting transfers between devices  19.1 us (5%)
  local copies, waits for them, and re-layouts  19 us (5%)
  between operations  15.2 us (4%)
    ppermute x10, waiting for transfers between devices, exchange(): return lax.ppermute(values, AXES, [(i, i ^ bit) for i in range(devices)])  69.1 us
    dot_general x9, matrix products, product_t(): lax.dot_general(left, right, (((1,), (1,)), ((), ())), preferred_element_...  45.1 us
    dot_general x9, matrix products, product(): return jnp.dot(left, right, preferred_element_type=jnp.float32)  38.6 us
    all_to_all x2, waiting for transfers between devices, all_to_all(): return lax.all_to_all(values, AXES, split_axis=0, concat_axis=0, tiled=True)  37.8 us
    pallas_call x1, Pallas kernels, attend_backward(): pl.pallas_call(attend_backward_kernel, out_shape=(shape, shape, shape), g...  34.4 us
    pallas_call x1, Pallas kernels, attend_forward(): pl.pallas_call(attend_forward_kernel, out_shape=(jax.ShapeDtypeStruct((ro...  22.2 us
    all_gather x1, waiting for transfers between devices, gather_rows(): rest = lax.all_gather(rows_of(homed[:, :split]), AXES, axis=0, tiled=True)  21.4 us
    all_to_all x1, blocking collectives, all_to_all(): return lax.all_to_all(values, AXES, split_axis=0, concat_axis=0, tiled=True)  20.2 us
  transfers between devices with their start and end apart: 14, of which 13 were waited for; matrix products, arithmetic and copies ran while one was open for 18% of the time, Pallas kernels for 14%

profile of v4, /device:TPU:0, one launch (start us, length us, event | category | flops | bytes accessed | tf_op | source)
XLA Modules:
  0.0 413.5 jit_solution(6318013133625686142)
XLA Ops:
  12.0 7.3 %all-to-all-start = ((bf16[32,40,384]{2,1,0:T(8,128)(2,1)}), bf16[32,40,384]{2,1,0:T(8,128)(2,1)S(1)}, u32[]{:S(2)}, u32[]{:S(2)}) async-start(bf16[32,40,384]{2,1,0:T(8,128)(2,1)} %pad_maximum_fusion.2), calls=%async_computation | async-start | bytes 1966080 | tf_op jit(solution)/shard_map/all_to_all | solution.py:277
  20.9 23.2 %all-to-all-done = bf16[32,40,384]{2,1,0:T(8,128)(2,1)S(1)} async-done(((bf16[32,40,384]{2,1,0:T(8,128)(2,1)}), bf16[32,40,384]{2,1,0:T(8,128)(2,1)S(1)}, u32[]{:S(2)}, u32[]{:S(2)}) %all-to-all-start) | async-done | bytes 983072 | tf_op jit(solution)/shard_map/all_to_all | solution.py:277
  49.4 20.2 %all_to_all.15 = bf16[32,20,288]{2,1,0:T(8,128)(2,1)S(1)} all-to-all(bf16[32,20,288]{2,1,0:T(8,128)(2,1)S(1)} %reshape.232), channel_id=1, replica_groups=mesh['rows'=8,'heads'=4] {'rows','heads'}, dimensions={0} | all-to-all | bytes 737280 | tf_op jit(solution)/shard_map/all_to_all | solution.py:277
  73.5 5.1 %convolution_convert_fusion = bf16[1024,1024]{1,0:T(8,128)(2,1)} fusion(bf16[1024,768]{1,0:T(8,128)(2,1)} %param.15, bf16[768,1024]{1,0:T(8,128)(2,1)} %param.21), kind=kOutput, calls=%fused_computation.70 | convolution fusion | flops 1611661312 | bytes 5242880 | tf_op jit(solution)/shard_map/dot_general | solution.py:42
  87.1 5.2 %collective-permute-done.1 = bf16[2,24,768]{2,1,0:T(8,128)(2,1)S(1)} collective-permute-done((bf16[2,24,768]{2,1,0:T(8,128)(2,1)S(1)}, bf16[2,24,768]{2,1,0:T(8,128)(2,1)S(1)}, u32[]{:S(2)}, u32[]{:S(2)}) %collective-permute-start.1) | collective-permute-done | bytes 73760 | tf_op jit(solution)/shard_map/ppermute | solution.py:243
  101.5 10.8 %collective-permute-done.3 = bf16[8,24,768]{2,1,0:T(8,128)(2,1)S(1)} collective-permute-done((bf16[8,24,768]{2,1,0:T(8,128)(2,1)S(1)}, bf16[8,24,768]{2,1,0:T(8,128)(2,1)S(1)}, u32[]{:S(2)}, u32[]{:S(2)}) %collective-permute-start.3) | collective-permute-done | bytes 294944 | tf_op jit(solution)/shard_map/ppermute | solution.py:243
  118.8 22.2 %attend_forward.1 = (bf16[1024,768]{1,0:T(8,128)(2,1)}, f32[6,2,1024]{2,1,0:T(2,128)}) custom-call(s32[3]{0:T(128)} %pad_add_fusion.1.spans, bf16[1024,768]{1,0:T(8,128)(2,1)} %add_convert_fusion.4.query_ref, bf16[1024,768]{1,0:T(8,128)(2,1)} %fusion.50.keys_ref, bf16[1024,768]{1,0:T(8,128)(2,1)} %add_convert_fusion.3.values_ref), custom_call_target="tpu_custom_call" | custom-call | tf_op jit(solution)/shard_map/attend_forward/pallas_call | solution.py:199
  141.0 21.4 %all-gather.2.cloned.1.call-done = bf16[6912,768]{1,0:T(8,128)(2,1)} async-done(((bf16[216,768]{1,0:T(8,128)(2,1)}), bf16[6912,768]{1,0:T(8,128)(2,1)}) %all-gather.2.cloned.1.call-update) | async-done | bytes 10616848 | tf_op jit(solution)/shard_map/all_gather | solution.py:404
  168.1 11.9 %fusion.4 = (bf16[1024,3072]{1,0:T(8,128)(2,1)S(1)}, bf16[1024,3072]{1,0:T(8,128)(2,1)S(1)}) fusion(f32[3072]{0:T(1024)S(1)} %slice_convert_fusion, bf16[1024,768]{1,0:T(8,128)(2,1)S(1)} %fusion.27.hidden_ref, bf16[6912,768]{1,0:T(8,128)(2,1)S(1)} %copy-done.35), kind=kOutput, calls=%fused_computation.5 | convolution fusion | flops 4869586944 | bytes 18886656 | tf_op jit(solution)/shard_map/dot_general | solution.py:46
  180.0 5.4 %fusion.75 = (f32[1024]{0:T(1024)S(1)}, f32[1024,768]{1,0:T(8,128)S(1)}) fusion(f32[768]{0:T(1024)S(1)} %get-tuple-element.61, bf16[1024,3072]{1,0:T(8,128)(2,1)S(1)} %get-tuple-element.18.active_ref, bf16[6912,768]{1,0:T(8,128)(2,1)S(1)} %copy-done.35, f32[768]{0:T(1024)S(1)} %get-tuple-element.62, f32[768]{0:T(1024)S(1)} %get-tuple-element.63, ...), kind=kOutput, calls=%fused_computation.170 | convolution fusion | flops 4837342208 | bytes 17326080 | tf_op jit(solution)/shard_map/dot_general | solution.py:42
  192.7 7.2 %fusion.76 = (bf16[3072]{0:T(1024)(128)(2,1)S(1)}, bf16[1024,3072]{1,0:T(8,128)(2,1)}) fusion(bf16[1024,3072]{1,0:T(8,128)(2,1)S(1)} %get-tuple-element.19, bf16[1024,768]{1,0:T(8,128)(2,1)S(1)} %get-tuple-element.42.branch_ref, bf16[6912,768]{1,0:T(8,128)(2,1)S(1)} %copy-done.35), kind=kOutput, calls=%fused_computation.171 | convolution fusion | flops 4844418048 | bytes 18880512 | tf_op jit(solution)/shard_map/dot_general | solution.py:46
  199.8 16.9 %weight_grads.1 = bf16[768,6144]{1,0:T(8,128)(2,1)} custom-call(bf16[1024,3072]{1,0:T(8,128)(2,1)} %get-tuple-element.76.pre_ref, bf16[1024,768]{1,0:T(8,128)(2,1)} %copy-done.11, bf16[1024,3072]{1,0:T(8,128)(2,1)} %copy-done.13, bf16[1024,768]{1,0:T(8,128)(2,1)} %copy-done.12), custom_call_target="tpu_custom_call" | custom-call | tf_op jit(solution)/shard_map/weight_grads/pallas_call | solution.py:435
  216.7 11.7 %multiply_reduce_fusion = (bf16[768]{0:T(1024)(128)(2,1)S(1)}, f32[1024]{0:T(1024)S(1)}, f32[1024]{0:T(1024)S(1)}, bf16[768]{0:T(1024)(128)(2,1)S(1)}, f32[1024,768]{1,0:T(8,128)S(1)}) fusion(f32[1024,768]{1,0:T(8,128)} %copy-done.2, f32[1024]{0:T(1024)S(1)} %add_rsqrt_fusion.1, f32[1024]{0:T(1024)S(1)} %broadcast_multiply_fusion.5, ...), kind=kOutput, calls=%fused_computation.42 | convolution fusion | flops 4845989888 | bytes 22062080 | tf_op jit(solution)/shard_map/dot_general | solution.py:42
  229.6 4.9 %convolution_convert_fusion.2.grad_ref = bf16[1024,768]{1,0:T(8,128)(2,1)} fusion(bf16[6912,768]{1,0:T(8,128)(2,1)} %all-gather.2.cloned.1.call-done, f32[1024,768]{1,0:T(8,128)S(1)} %get-tuple-element.44), kind=kOutput, calls=%fused_computation.73 | convolution fusion | flops 1209532416 | bytes 5898240 | tf_op jit(solution)/shard_map/dot_general | solution.py:46
  234.5 34.4 %attend_backward.1 = (bf16[1024,768]{1,0:T(8,128)(2,1)}, bf16[1024,768]{1,0:T(8,128)(2,1)}, bf16[1024,768]{1,0:T(8,128)(2,1)}) custom-call(s32[3]{0:T(128)} %pad_add_fusion.1.spans, bf16[1024,768]{1,0:T(8,128)(2,1)} %add_convert_fusion.4.query_ref, bf16[1024,768]{1,0:T(8,128)(2,1)} %fusion.50.keys_ref, bf16[1024,768]{1,0:T(8,128)(2,1)} %add_convert_fusion.3.values_ref, ...), custom_call_target="tpu_custom_call" | custom-call | tf_op jit(solution)/shard_map/attend_backward/pallas_call | solution.py:221
  272.3 4.1 fusion.8
  293.4 22.2 %collective-permute-done.6 = bf16[8,56,768]{2,1,0:T(8,128)(2,1)S(1)} collective-permute-done((bf16[8,56,768]{2,1,0:T(8,128)(2,1)S(1)}, bf16[8,56,768]{2,1,0:T(8,128)(2,1)S(1)}, u32[]{:S(2)}, u32[]{:S(2)}) %collective-permute-start.6) | collective-permute-done | bytes 688160 | tf_op jit(solution)/shard_map/ppermute | solution.py:243
  318.1 14.2 %collective-permute-done.7 = bf16[4,56,768]{2,1,0:T(8,128)(2,1)S(1)} collective-permute-done((bf16[4,56,768]{2,1,0:T(8,128)(2,1)S(1)}, bf16[4,56,768]{2,1,0:T(8,128)(2,1)S(1)}, u32[]{:S(2)}, u32[]{:S(2)}) %collective-permute-start.7) | collective-permute-done | bytes 344096 | tf_op jit(solution)/shard_map/ppermute | solution.py:243
  336.1 7.4 %collective-permute-done.8 = bf16[2,56,768]{2,1,0:T(8,128)(2,1)S(1)} collective-permute-done((bf16[2,56,768]{2,1,0:T(8,128)(2,1)S(1)}, bf16[2,56,768]{2,1,0:T(8,128)(2,1)S(1)}, u32[]{:S(2)}, u32[]{:S(2)}) %collective-permute-start.8) | collective-permute-done | bytes 172064 | tf_op jit(solution)/shard_map/ppermute | solution.py:243
  349.7 14.4 %reduce-scatter.2.cloned.1.call-done.wide_ref = bf16[24,6144]{1,0:T(8,128)(2,1)} async-done(((bf16[768,6144]{1,0:T(8,128)(2,1)}), bf16[24,6144]{1,0:T(8,128)(2,1)}) %reduce-scatter.2.cloned.1.call-update) | async-done | bytes 294928 | tf_op jit(solution)/shard_map/reduce_scatter | solution.py:462
  364.1 4.4 %place.1 = bf16[1280,288]{1,0:T(8,128)(2,1)} custom-call(bf16[24,6144]{1,0:T(8,128)(2,1)} %reduce-scatter.2.cloned.1.call-done.wide_ref, bf16[56,768]{1,0:T(8,128)(2,1)} %bitcast.157, s32[1,640]{1,0:T(1,128)} %broadcast_in_dim.5.slot_ref), custom_call_target="tpu_custom_call" | custom-call | tf_op jit(solution)/shard_map/place/pallas_call | solution.py:372
  376.9 4.2 %add_convert_fusion.1 = bf16[1024,768]{1,0:T(8,128)(2,1)} fusion(f32[1024,768]{1,0:T(8,128)S(1)} %copy-done.10, f32[1024,768]{1,0:T(8,128)S(1)} %fusion.78, f32[1024,768]{1,0:T(8,128)S(1)} %copy-done.9, f32[1024,768]{1,0:T(8,128)S(1)} %copy-done.20, bf16[1024,768]{1,0:T(8,128)(2,1)} %get-tuple-element.22, bf16[768,768]{1,0:T(8,128)(2,1)S(1)} %bitcast.141), kind=kOutput, calls=%fused_computation.43 | convolution fusion | flops 1211891712 | bytes 16908288 | tf_op jit(solution)/shard_map/dot_general | solution.py:46
  382.6 14.6 %all-to-all-done.2.pieces_ref = bf16[32,40,288]{2,1,0:T(8,128)(2,1)} async-done(((bf16[32,40,288]{2,1,0:T(8,128)(2,1)}), bf16[32,40,288]{2,1,0:T(8,128)(2,1)}, u32[]{:S(2)}, u32[]{:S(2)}) %all-to-all-start.2) | async-done | bytes 737312 | tf_op jit(solution)/shard_map/all_to_all | solution.py:277
  401.0 5.4 %fusion.70 = (bf16[480,768]{1,0:T(8,128)(2,1)}, f32[480,768]{1,0:T(8,128)}, f32[480,768]{1,0:T(8,128)}, f32[480,768]{1,0:T(8,128)}) fusion(f32[480,768]{1,0:T(8,128)S(1)} %copy-done.16, f32[480,768]{1,0:T(8,128)} %assemble.1, f32[480,768]{1,0:T(8,128)} %param.25, f32[480,768]{1,0:T(8,128)} %param.26), kind=kLoop, calls=%fused_computation.167 | loop fusion | flops 5529600 | bytes 11059200 | tf_op jit(solution)/shard_map/convert_element_type | solution.py:617
  (204 shorter events, 99.8 us)
Async XLA Ops:
  7.2 73.2 %copy-start = (bf16[1024,768]{1,0:T(8,128)(2,1)S(1)}, bf16[1024,768]{1,0:T(8,128)(2,1)}, u32[]{:S(2)}) copy-start(bf16[1024,768]{1,0:T(8,128)(2,1)} %param.22) | copy-start | bytes 4718596
  12.0 32.1 %all-to-all-start = ((bf16[32,40,384]{2,1,0:T(8,128)(2,1)}), bf16[32,40,384]{2,1,0:T(8,128)(2,1)S(1)}, u32[]{:S(2)}, u32[]{:S(2)}) async-start(bf16[32,40,384]{2,1,0:T(8,128)(2,1)} %pad_maximum_fusion.2), calls=%async_computation | async-start | bytes 1966080 | tf_op jit(solution)/shard_map/all_to_all | solution.py:277
  19.3 143.0 %all-gather.2.cloned.1.call-start = ((), (), s32[]{:S(2)}) async-start(), calls=%async_computation.4 | async-start | bytes 10948608 | tf_op jit(solution)/shard_map/all_gather | solution.py:404
  48.2 23.3 %copy-start.34 = (s32[4,2]{0,1:T(2,128)S(1)}, s32[4,2]{0,1:T(2,128)}, u32[]{:S(2)}) copy-start(s32[4,2]{0,1:T(2,128)} %param.17) | copy-start | bytes 100
  48.2 23.5 %copy-start.41 = (s32[4]{0:T(128)S(1)}, s32[4]{0:T(128)}, u32[]{:S(2)}) copy-start(s32[4]{0:T(128)} %param.18) | copy-start | bytes 52
  71.2 292.9 %reduce-scatter.2.cloned.1.call-start = ((), (), s32[]{:S(2)}) async-start(), calls=%async_computation.5 | async-start | bytes 9732096 | tf_op jit(solution)/shard_map/reduce_scatter | solution.py:462
  79.9 6.9 %collective-permute-start = (bf16[1,24,768]{2,1,0:T(8,128)(2,1)S(1)}, bf16[1,24,768]{2,1,0:T(8,128)(2,1)S(1)}, u32[]{:S(2)}, u32[]{:S(2)}) collective-permute-start(bf16[1,24,768]{2,1,0:T(8,128)(2,1)S(1)} %broadcast_in_dim_reshape.7), channel_id=1, source_target_pairs={{0,16},{1,17},{2,18},{3,19},{4,20},{5,21},{6,22},{7,23},{8,24},{9,... | collective-permute-start | bytes 110600 | tf_op jit(solution)/shard_map/ppermute | solution.py:243
  86.9 5.5 %collective-permute-start.1 = (bf16[2,24,768]{2,1,0:T(8,128)(2,1)S(1)}, bf16[2,24,768]{2,1,0:T(8,128)(2,1)S(1)}, u32[]{:S(2)}, u32[]{:S(2)}) collective-permute-start(bf16[2,24,768]{2,1,0:T(8,128)(2,1)S(1)} %bitcast.158), channel_id=1, source_target_pairs={{0,8},{1,9},{2,10},{3,11},{4,12},{5,13},{6,14},{7,15},{8,0},{9,1},... | collective-permute-start | bytes 221192 | tf_op jit(solution)/shard_map/ppermute | solution.py:243
  92.4 5.2 %collective-permute-start.2 = (bf16[4,24,768]{2,1,0:T(8,128)(2,1)S(1)}, bf16[4,24,768]{2,1,0:T(8,128)(2,1)S(1)}, u32[]{:S(2)}, u32[]{:S(2)}) collective-permute-start(bf16[4,24,768]{2,1,0:T(8,128)(2,1)S(1)} %bitcast.155), channel_id=1, source_target_pairs={{0,4},{1,5},{2,6},{3,7},{4,0},{5,1},{6,2},{7,3},{8,12},{9,13},{10,... | collective-permute-start | bytes 442376 | tf_op jit(solution)/shard_map/ppermute | solution.py:243
  97.6 14.7 %collective-permute-start.3 = (bf16[8,24,768]{2,1,0:T(8,128)(2,1)S(1)}, bf16[8,24,768]{2,1,0:T(8,128)(2,1)S(1)}, u32[]{:S(2)}, u32[]{:S(2)}) collective-permute-start(bf16[8,24,768]{2,1,0:T(8,128)(2,1)S(1)} %bitcast.151), channel_id=1, source_target_pairs={{0,2},{1,3},{2,0},{3,1},{4,6},{5,7},{6,4},{7,5},{8,10},{9,11},{10,... | collective-permute-start | bytes 884744 | tf_op jit(solution)/shard_map/ppermute | solution.py:243
  101.5 13.6 %copy-start.22 = (f32[1024,768]{1,0:T(8,128)}, f32[1024,768]{1,0:T(8,128)S(1)}, u32[]{:S(2)}) copy-start(f32[1024,768]{1,0:T(8,128)S(1)} %fusion.32) | copy-start | bytes 9437188
  112.4 2.7 collective-permute-start.4
  118.8 43.5 %copy-start.37 = (bf16[1024,768]{1,0:T(8,128)(2,1)S(1)}, bf16[1024,768]{1,0:T(8,128)(2,1)}, u32[]{:S(2)}) copy-start(bf16[1024,768]{1,0:T(8,128)(2,1)} %param.15) | copy-start | bytes 4718596
  165.8 14.2 %copy-start.2 = (f32[1024,768]{1,0:T(8,128)}, f32[1024,768]{1,0:T(8,128)S(1)}, u32[]{:S(2)}) copy-start(f32[1024,768]{1,0:T(8,128)S(1)} %get-tuple-element.70) | copy-start | bytes 9437188
  288.1 3.2 collective-permute-start.5
  291.3 41.2 %copy-start.6 = (f32[1024,1024]{1,0:T(8,128)S(1)}, f32[1024,1024]{1,0:T(8,128)}, u32[]{:S(2)}) copy-start(f32[1024,1024]{1,0:T(8,128)} %get-tuple-element.74) | copy-start | bytes 12582916
  291.9 40.6 %copy-start.28 = (bf16[768,1024]{1,0:T(8,128)(2,1)S(1)}, bf16[768,1024]{1,0:T(8,128)(2,1)}, u32[]{:S(2)}) copy-start(bf16[768,1024]{1,0:T(8,128)(2,1)} %param.21) | copy-start | bytes 4718596
  292.0 40.6 %copy-start.5 = (f32[1024,1024]{1,0:T(8,128)S(1)}, f32[1024,1024]{1,0:T(8,128)}, u32[]{:S(2)}) copy-start(f32[1024,1024]{1,0:T(8,128)} %copy-done.4) | copy-start | bytes 12582916
  292.0 23.6 %collective-permute-start.6 = (bf16[8,56,768]{2,1,0:T(8,128)(2,1)S(1)}, bf16[8,56,768]{2,1,0:T(8,128)(2,1)S(1)}, u32[]{:S(2)}, u32[]{:S(2)}) collective-permute-start(bf16[8,56,768]{2,1,0:T(8,128)(2,1)S(1)} %fusion.55), channel_id=1, source_target_pairs={{0,2},{1,3},{2,0},{3,1},{4,6},{5,7},{6,4},{7,5},{8,10},{9,11},{10,... | collective-permute-start | bytes 2064392 | tf_op jit(solution)/shard_map/ppermute | solution.py:243
  316.0 16.3 %collective-permute-start.7 = (bf16[4,56,768]{2,1,0:T(8,128)(2,1)S(1)}, bf16[4,56,768]{2,1,0:T(8,128)(2,1)S(1)}, u32[]{:S(2)}, u32[]{:S(2)}) collective-permute-start(bf16[4,56,768]{2,1,0:T(8,128)(2,1)S(1)} %fusion.58), channel_id=1, source_target_pairs={{0,4},{1,5},{2,6},{3,7},{4,0},{5,1},{6,2},{7,3},{8,12},{9,13},{10,... | collective-permute-start | bytes 1032200 | tf_op jit(solution)/shard_map/ppermute | solution.py:243
  332.4 11.1 %collective-permute-start.8 = (bf16[2,56,768]{2,1,0:T(8,128)(2,1)S(1)}, bf16[2,56,768]{2,1,0:T(8,128)(2,1)S(1)}, u32[]{:S(2)}, u32[]{:S(2)}) collective-permute-start(bf16[2,56,768]{2,1,0:T(8,128)(2,1)S(1)} %select_bitcast_fusion.1), channel_id=1, source_target_pairs={{0,8},{1,9},{2,10},{3,11},{4,12},{5,13},{6,14},{7,15},{8,0},{9,1},... | collective-permute-start | bytes 516104 | tf_op jit(solution)/shard_map/ppermute | solution.py:243
  343.6 5.4 %collective-permute-start.9 = (bf16[1,56,768]{2,1,0:T(8,128)(2,1)S(1)}, bf16[1,56,768]{2,1,0:T(8,128)(2,1)S(1)}, u32[]{:S(2)}, u32[]{:S(2)}) collective-permute-start(bf16[1,56,768]{2,1,0:T(8,128)(2,1)S(1)} %select_bitcast_fusion.2), channel_id=1, source_target_pairs={{0,16},{1,17},{2,18},{3,19},{4,20},{5,21},{6,22},{7,23},{8,24},{9,... | collective-permute-start | bytes 258056 | tf_op jit(solution)/shard_map/ppermute | solution.py:243
  368.5 28.7 %all-to-all-start.2 = ((bf16[32,40,288]{2,1,0:T(8,128)(2,1)}), bf16[32,40,288]{2,1,0:T(8,128)(2,1)}, u32[]{:S(2)}, u32[]{:S(2)}) async-start(bf16[32,40,288]{2,1,0:T(8,128)(2,1)} %bitcast.143), calls=%async_computation.3 | async-start | bytes 1966080 | tf_op jit(solution)/shard_map/all_to_all | solution.py:277
  381.1 19.9 %copy-start.16 = (f32[480,768]{1,0:T(8,128)S(1)}, f32[480,768]{1,0:T(8,128)}, u32[]{:S(2)}) copy-start(f32[480,768]{1,0:T(8,128)} %param.24) | copy-start | bytes 4423684
  (32 other events, 201.5 us)
Sparse Core Ops, SparseCore 0:
  71.4 90.9 all-gather.1
  216.8 147.2 reduce-scatter.1
